TPU v7x, 32 devices: a whole 2x2x4 slice. The times are simulated.
32 devices in a mesh: pi: 4 (over x, core), pj: 8 (over z, y).
Axes of the slice: x: 2, y: 2, z: 4, core: 2. Of those that a mesh axis runs over, the one named last changes fastest.
Arguments:
- amplitudes: bfloat16 [8, 8, 128, 128], P('pi', 'pj'), may hold values from -6 to 6
- cholesky: bfloat16 [128, 128, 4096], P(None, None, 'pj'), may hold values from -1 to 1, as said below
- other_terms: float32 [8, 8, 128, 128], P('pi', 'pj'), may hold values from -6 to 6
Outputs:
- residual: float32 [8, 8, 128, 128], P('pi', 'pj')
Inputs may be any that keep to these rules, and one draw needn't show every extreme that they name: cholesky[x, y, P] equals cholesky[y, x, P].
All inputs are finite; a program needn't handle non-finite values.
Results may differ from a plain program's by a relative error of at most 0.0036.
Values may be sent and summed in bfloat16 or wider, within the bound.
No kernel may reach another device: no remote copies, remote signals or barrier semaphores. Data moves between devices by JAX's collectives and lax.ppermute only.
A program may use at most 128 MiB of HBM per device.

v0:
```python
import jax
import jax.numpy as jnp
from jax import lax
from jax.sharding import PartitionSpec as P


def from_partner(block, axis, apart):
    count = lax.axis_size(axis)
    route = []
    for low in range(count):
        high = low | 1 << apart
        if high != low and high < count:
            route += [(low, high), (high, low)]
    return lax.ppermute(block, axis, route)


def product(left, right):
    return jnp.einsum("cap,bdp->abcd", left, right, preferred_element_type=jnp.float32)


def ladder_rows(source, flat, tile_shape, count):
    inner = source.shape[1]
    matrix = source.reshape(count * inner, -1)
    result = lax.dot_general(
        matrix, flat, (((1,), (1,)), ((), ())), preferred_element_type=jnp.float32
    )
    return result.reshape(count, inner, tile_shape[0], tile_shape[1])


def shards(amplitudes, cholesky, other_terms):
    width = cholesky.shape[0]
    pair_i = amplitudes.shape[0]
    pair_j = amplitudes.shape[1]
    count_i = lax.axis_size("pi")
    block_i = width // count_i
    row_index = lax.axis_index("pi")
    col_index = lax.axis_index("pj")
    from_j = lax.all_to_all(cholesky, "pj", split_axis=0, concat_axis=2, tiled=True)
    own_rows = lax.dynamic_slice_in_dim(cholesky, row_index * block_i, block_i, 0)
    from_i = lax.all_gather(own_rows, "pj", axis=2, tiled=True)
    total = product(from_i, from_j)
    tile = total.astype(jnp.bfloat16)
    tile_shape = (tile.shape[0], tile.shape[1])
    flat = tile.reshape(tile.shape[0] * tile.shape[1], tile.shape[2] * tile.shape[3])
    split = lax.all_to_all(amplitudes, "pi", split_axis=2, concat_axis=0, tiled=True)
    gathered = lax.all_gather(split, "pj", axis=1, tiled=True)
    sums = lax.psum_scatter(
        ladder_rows(gathered, flat, tile_shape, lax.axis_size("pi") * pair_i),
        "pi",
        scatter_dimension=0,
        tiled=True,
    )
    ladder = lax.all_to_all(sums, "pj", split_axis=1, concat_axis=3, tiled=True)
    half = (other_terms + 0.5 * ladder).astype(jnp.bfloat16)
    halves = half.reshape(2, pair_j, pair_j, width, width)
    parity = col_index % 2
    retained = jnp.where(parity == 0, halves[0], halves[1])
    outgoing = jnp.where(parity == 0, halves[1], halves[0])
    received = from_partner(outgoing, "pj", 0)
    buffer = jnp.where(
        parity == 0, jnp.stack([retained, received]), jnp.stack([received, retained])
    )
    upper = col_index // 2
    levels = count_i.bit_length() - 1
    for level in range(levels):
        across = from_partner(buffer, "pi", level)
        across = from_partner(across, "pj", level + 1)
        differ = row_index // 2**level % 2 != upper // 2**level % 2
        buffer = jnp.where(differ, across, buffer)
    mirrored = jnp.transpose(buffer, (0, 2, 1, 4, 3)).reshape(pair_i, pair_j, width, width)
    return half.astype(jnp.float32) + mirrored.astype(jnp.float32)


def solution(mesh):
    return jax.shard_map(
        shards,
        mesh=mesh,
        in_specs=(P("pi", "pj", None, None), P(None, None, "pj"), P("pi", "pj", None, None)),
        out_specs=P("pi", "pj", None, None),
        check_vma=False,
    )
```

profile of v0, /device:TPU:0, one launch (start us, length us, event | category | flops | bytes accessed | tf_op | source)
XLA Modules:
  0.0 1056.7 jit_solution(2526487211110519490)
XLA Ops:
  6.5 0.0 all-gather.2.cloned.1.call-start
  6.5 4.6 constant_dynamic-slice_fusion
  11.2 0.0 all-gather.2.cloned.1.call-update
  11.2 0.9 copy.27
  12.1 8.2 all_to_all.45
  20.2 5.9 all-to-all-start
  26.2 0.0 reduce-scatter.2.cloned.1.call-start
  26.3 627.4 %all_gather.7 = bf16[8,8,32,128]{3,2,0,1:T(8,128)(2,1)S(1)} all-gather(bf16[8,1,32,128]{3,2,0,1:T(8,128)(2,1)S(1)} %bitcast.67), channel_id=1, replica_groups=mesh['pi'=4,'pj'=8] {'pj'}, dimensions={1}, use_global_device_ids=true | all-gather | bytes 589824 | tf_op jit(solution)/shard_map/all_gather | solution.py:46
  653.7 0.8 copy.57
  654.6 0.0 all-to-all-done
  654.6 18.5 %copy.56 = bf16[8,16,128,512]{3,0,2,1:T(8,128)(2,1)} copy(bf16[8,16,128,512]{3,2,1,0:T(8,128)(2,1)} %bitcast.2) | data formatting | bytes 33554432 | tf_op jit(solution)/shard_map/all_to_all | solution.py:38
  673.1 25.7 %reshape.118 = bf16[16,128,4096,1]{2,1,0,3:T(8,128)(2,1)} reshape(bf16[16,128,8,512]{3,2,1,0:T(8,128)(2,1)} %bitcast.63) | data formatting | bytes 33554432 | tf_op jit(solution)/shard_map/all_to_all | solution.py:38
  698.7 142.6 %all-gather.2.cloned.1.call-done = bf16[32,128,4096]{2,1,0:T(8,128)(2,1)} async-done(((bf16[32,128,512]{2,1,0:T(8,128)(2,1)}), bf16[32,128,4096]{2,1,0:T(8,128)(2,1)}) %all-gather.2.cloned.1.call-update) | async-done | bytes 33554448 | tf_op jit(solution)/shard_map/all_gather | solution.py:40
  841.3 78.1 %convert_bitcast_fusion = bf16[128,16,32,128]{3,0,1,2:T(8,128)(2,1)} fusion(bf16[16,128,4096,1]{2,1,0,3:T(8,128)(2,1)} %reshape.118, bf16[32,128,4096]{2,1,0:T(8,128)(2,1)} %all-gather.2.cloned.1.call-done), kind=kOutput, calls=%fused_computation.6 | convolution fusion | flops 68727865344 | bytes 67108864 | tf_op jit(solution)/shard_map/cap,bdp->abcd/dot_general | solution.py:18
  919.4 0.0 copy-start
  919.4 15.0 %copy.26 = bf16[128,16,32,128]{3,2,1,0:T(8,128)(2,1)S(1)} copy(bf16[128,16,32,128]{3,0,1,2:T(8,128)(2,1)} %convert_bitcast_fusion) | data formatting | bytes 33554432 | tf_op jit(solution)/shard_map/convert_element_type | solution.py:42
  934.4 0.0 copy-done
  934.4 0.0 copy-start.1
  934.4 9.0 fusion.7
  943.5 2.8 reshape.115
  946.3 0.0 reduce-scatter.2.cloned.1.call-update
  946.3 68.4 %reduce-scatter.2.cloned.1.call-done = f32[2,8,128,16]{3,2,1,0:T(8,128)} async-done(((f32[8,8,128,16]{3,2,1,0:T(8,128)}), f32[2,8,128,16]{3,2,1,0:T(8,128)}) %reduce-scatter.2.cloned.1.call-update) | async-done | bytes 131088 | tf_op jit(solution)/shard_map/reduce_scatter | solution.py:47
  1014.7 2.2 copy.31
  1016.9 5.5 all-to-all-start.2
  1022.4 0.0 copy-done.1
  1022.4 0.1 copy.33
  1022.5 7.2 all-to-all-done.2
  1029.8 0.3 collective-permute-start
  1030.0 3.7 collective-permute-done
  1033.8 0.1 collective-permute-start.1
  1033.8 1.2 collective-permute-done.1
  1035.1 0.0 collective-permute-start.2
  1035.1 4.3 collective-permute-done.2
  1039.4 0.6 collective-permute-start.3
  1040.0 3.7 collective-permute-done.3
  1043.7 0.4 collective-permute-start.4
  1044.1 0.1 copy.34
  1044.2 5.0 collective-permute-done.4
  1049.2 0.7 fusion.12
  (8 shorter events, 0.1 us)
Async XLA Ops:
  6.5 834.8 %all-gather.2.cloned.1.call-start = ((), (), s32[]{:S(2)}) async-start(), calls=%async_computation.4 | async-start | bytes 37748736 | tf_op jit(solution)/shard_map/all_gather | solution.py:40
  20.2 634.3 %all-to-all-start = ((bf16[128,128,512]{2,1,0:T(8,128)(2,1)}), bf16[128,128,512]{2,1,0:T(8,128)(2,1)}, u32[]{:S(2)}, u32[]{:S(2)}) async-start(bf16[128,128,512]{2,1,0:T(8,128)(2,1)} %param.4), calls=%async_computation | async-start | bytes 33554432 | tf_op jit(solution)/shard_map/all_to_all | solution.py:38
  26.2 988.5 %reduce-scatter.2.cloned.1.call-start = ((), (), s32[]{:S(2)}) async-start(), calls=%async_computation.5 | async-start | bytes 5242880 | tf_op jit(solution)/shard_map/reduce_scatter | solution.py:47
  919.4 15.0 %copy-start = (bf16[8,8,32,128]{3,2,1,0:T(8,128)(2,1)S(1)}, bf16[8,8,32,128]{3,2,1,0:T(8,128)(2,1)}, u32[]{:S(2)}) copy-start(bf16[8,8,32,128]{3,2,1,0:T(8,128)(2,1)} %copy.57) | copy-start | bytes 1572868
  934.4 87.9 %copy-start.1 = (f32[2,1,128,128]{3,2,1,0:T(8,128)S(1)}, f32[2,1,128,128]{3,2,1,0:T(8,128)}, u32[]{:S(2)}) copy-start(f32[2,1,128,128]{3,2,1,0:T(8,128)} %param.5) | copy-start | bytes 393220
  1016.9 12.9 %all-to-all-start.2 = ((f32[2,8,128,16]{2,3,0,1:T(8,128)}), f32[2,8,128,16]{2,3,0,1:T(8,128)S(1)}, u32[]{:S(2)}, u32[]{:S(2)}) async-start(f32[2,8,128,16]{2,3,0,1:T(8,128)} %copy.31), calls=%async_computation.3 | async-start | bytes 262144 | tf_op jit(solution)/shard_map/all_to_all | solution.py:53
  1029.8 4.0 collective-permute-start
  1033.8 1.3 collective-permute-start.1
  1035.1 4.3 collective-permute-start.2
  1039.4 4.3 collective-permute-start.3
  1043.7 5.5 collective-permute-start.4
Sparse Core Ops, SparseCore 0:
  11.3 829.9 all-gather.1
  946.4 68.2 reduce-scatter.1
where the time goes:
time: 1060 us
  blocking collectives  636 us (60%)
  waiting for transfers between devices  236 us (22%)
  matrix products  87.1 us (8%)
  local copies, waits for them, and re-layouts  70.7 us (7%)
  between operations  13.5 us (1%)
  starting transfers between devices  12.9 us (1%)
    all_gather x1, blocking collectives, shards(): gathered = lax.all_gather(split, 'pj', axis=1, tiled=True)  627 us
    all_gather x1, waiting for transfers between devices, shards(): from_i = lax.all_gather(own_rows, 'pj', axis=2, tiled=True)  143 us
    dot_general x1, matrix products, product(): jnp.einsum('cap,bdp->abcd', left, right, preferred_element_type=jnp.float32)  78.1 us
    reduce_scatter x1, waiting for transfers between devices, shards(): lax.psum_scatter(ladder_rows(gathered, flat, tile_shape, lax.axis_size('p...  68.4 us
    all_to_all x2, local copies, waits for them, and re-layouts, shards(): lax.all_to_all(cholesky, 'pj', split_axis=0, concat_axis=2, tiled=True)  44.2 us
  transfers between devices with their start and end apart: 9, of which 8 were waited for; matrix products, arithmetic and copies ran while one was open for 4% of the time, Pallas kernels for 0%

commit v1 on v0

v1 whole, which is shorter than its diff:
```python
import functools

import jax
import jax.numpy as jnp
from jax import lax
from jax.experimental import pallas as pl
from jax.experimental.pallas import tpu as pltpu
from jax.sharding import PartitionSpec as P


BOTH = ("pi", "pj")
GROUP = 16
NT = (((1,), (1,)), ((), ()))
NN = (((1,), (0,)), ((), ()))
ANY = pl.BlockSpec(memory_space=pl.ANY)
VMEM = pl.BlockSpec(memory_space=pltpu.VMEM)


def mirrored(block):
    pair_i = block.shape[0]
    count_i, count_j = lax.axis_size("pi"), lax.axis_size("pj")
    col = lax.axis_index("pj")
    arrived = []
    for shift in range(pair_i):
        route = []
        for row in range(count_i):
            for at in range(count_j):
                to = (at // pair_i) * count_j + pair_i * row + (at + shift) % pair_i
                route.append((row * count_j + at, to))
        sent = lax.dynamic_index_in_dim(block, (col + shift) % pair_i, 0, keepdims=False)
        arrived.append(lax.ppermute(sent, BOTH, route))
    stacked = jnp.stack(arrived)
    return jnp.stack(
        [
            lax.dynamic_index_in_dim(stacked, (col - slot) % pair_i, 0, keepdims=False)
            for slot in range(pair_i)
        ]
    )


def packed(pairs):
    width = pairs.shape[-1]
    total = jnp.swapaxes(pairs, 1, 2).astype(jnp.float32) + mirrored(pairs).astype(jnp.float32)
    d = lax.broadcasted_iota(jnp.int32, (width, width), 0)
    c = lax.broadcasted_iota(jnp.int32, (width, width), 1)
    weight = jnp.where(c < d, 1.0, jnp.where(c == d, 0.5, 0.0))
    total = (total * weight).astype(jnp.bfloat16)
    parts = []
    for low in range(0, width, GROUP):
        high = low + GROUP
        parts.append(total[:, low:high, :high].reshape(pairs.shape[0], GROUP * high))
    return jnp.concatenate(parts, axis=1)


def offsets(width):
    at = [0]
    for k in range(width // GROUP):
        at.append(at[-1] + GROUP * GROUP * (k + 1))
    return at


def load(start, rows, l_hbm, own, vectors, sems):
    blocks = vectors.shape[0] // GROUP
    copies = [pltpu.make_async_copy(l_hbm.at[pl.ds(start, rows)], own, sems.at[blocks])]
    for k in range(blocks):
        part = pl.ds(k * GROUP, GROUP)
        copies.append(pltpu.make_async_copy(l_hbm.at[part], vectors.at[part], sems.at[k]))
    for copy in copies:
        copy.start()
    return copies


def form(own, vectors, at, chunk, k, store):
    width, _, depth = vectors.shape
    high = GROUP * (k + 1)
    left = own[pl.ds(at * chunk, chunk), :high, :].reshape(chunk * high, depth)
    for pair in range(0, GROUP, 2):
        right = vectors[pl.ds(k * GROUP + pair, 2)].reshape(2 * width, depth)
        product = lax.dot_general(left, right, NT, preferred_element_type=jnp.float32)
        product = product.astype(jnp.bfloat16)
        for q in range(2):
            part = product[:, q * width : (q + 1) * width].reshape(chunk, high, width)
            store(pl.ds((pair + q) * high, high), part)


def tile_kernel(rows, chunk, start_ref, l_hbm, t_hbm, vectors, own, tile, sems, sent):
    width = vectors.shape[0]
    blocks = width // GROUP
    at_row = offsets(width)
    copies = load(start_ref[0], rows, l_hbm, own, vectors, sems)
    copies[0].wait()

    def out_copy(at, k):
        size = at_row[k + 1] - at_row[k]
        return pltpu.make_async_copy(
            tile.at[k % 2, :, pl.ds(0, size)],
            t_hbm.at[pl.ds(at * chunk, chunk), pl.ds(at_row[k], size)],
            sent.at[k % 2],
        )

    def step(at, carry):
        for k in range(blocks):
            pl.when(at == 0)(copies[k + 1].wait)
            if k >= 2:
                out_copy(at, k - 2).wait()
            else:
                pl.when(at > 0)(out_copy(at - 1, blocks - 2 + k).wait)

            def store(part, value, k=k):
                tile[k % 2, :, part] = value

            form(own, vectors, at, chunk, k, store)
            out_copy(at, k).start()
        return carry

    lax.fori_loop(0, rows // chunk, step, 0)
    last = rows // chunk - 1
    out_copy(last, blocks - 2).wait()
    out_copy(last, blocks - 1).wait()


def tiles(cholesky, start, rows):
    width, _, depth = cholesky.shape
    chunk = min(8, rows)
    size = offsets(width)[-1]
    return pl.pallas_call(
        functools.partial(tile_kernel, rows, chunk),
        out_shape=jax.ShapeDtypeStruct((rows, size, width), jnp.bfloat16),
        grid_spec=pltpu.PrefetchScalarGridSpec(
            num_scalar_prefetch=1,
            grid=(),
            in_specs=[ANY],
            out_specs=ANY,
            scratch_shapes=[
                pltpu.VMEM((width, width, depth), jnp.bfloat16),
                pltpu.VMEM((rows, width, depth), jnp.bfloat16),
                pltpu.VMEM((2, chunk, GROUP * width, width), jnp.bfloat16),
                pltpu.SemaphoreType.DMA((width // GROUP + 1,)),
                pltpu.SemaphoreType.DMA((2,)),
            ],
        ),
        compiler_params=pltpu.CompilerParams(vmem_limit_bytes=56 << 20),
        cost_estimate=pl.CostEstimate(
            flops=2 * rows * width * size * depth,
            bytes_accessed=2 * width * width * depth + 2 * rows * size * width,
            transcendentals=0,
        ),
    )(start, cholesky)


def apply_kernel(t_ref, s_ref, out_ref):
    for a in range(t_ref.shape[0]):
        out_ref[a] = lax.dot_general(s_ref[...], t_ref[a], NN, preferred_element_type=jnp.float32)


def applied(tile, weights):
    rows, size, width = tile.shape
    pairs = weights.shape[0]
    each = 2 if rows % 2 == 0 else 1
    return pl.pallas_call(
        apply_kernel,
        out_shape=jax.ShapeDtypeStruct((rows, pairs, width), jnp.float32),
        grid=(rows // each,),
        in_specs=[pl.BlockSpec((each, size, width), lambda a: (a, 0, 0)), VMEM],
        out_specs=pl.BlockSpec((each, pairs, width), lambda a: (a, 0, 0)),
        compiler_params=pltpu.CompilerParams(vmem_limit_bytes=56 << 20),
        cost_estimate=pl.CostEstimate(
            flops=2 * rows * width * size * pairs,
            bytes_accessed=2 * rows * size * width,
            transcendentals=0,
        ),
    )(tile, weights)


def ladder_kernel(rows, chunk, start_ref, l_hbm, s_ref, out_ref, vectors, own, tile, sems):
    width = vectors.shape[0]
    blocks = width // GROUP
    at_row = offsets(width)
    copies = load(start_ref[0], rows, l_hbm, own, vectors, sems)
    copies[0].wait()

    def step(at, carry):
        for k in range(blocks):
            pl.when(at == 0)(copies[k + 1].wait)

            def store(part, value):
                tile[:, part] = value

            form(own, vectors, at, chunk, k, store)
            weights = s_ref[:, at_row[k] : at_row[k + 1]]
            for a in range(chunk):
                value = lax.dot_general(
                    weights,
                    tile[a, : at_row[k + 1] - at_row[k], :],
                    NN,
                    preferred_element_type=jnp.float32,
                )
                if k == 0:
                    out_ref[at * chunk + a] = value
                else:
                    out_ref[at * chunk + a] += value
        return carry

    lax.fori_loop(0, rows // chunk, step, 0)


def ladder(cholesky, weights, start, rows):
    width, _, depth = cholesky.shape
    pairs, size = weights.shape
    chunk = min(8, rows)
    return pl.pallas_call(
        functools.partial(ladder_kernel, rows, chunk),
        out_shape=jax.ShapeDtypeStruct((rows, pairs, width), jnp.float32),
        grid_spec=pltpu.PrefetchScalarGridSpec(
            num_scalar_prefetch=1,
            grid=(),
            in_specs=[ANY, VMEM],
            out_specs=VMEM,
            scratch_shapes=[
                pltpu.VMEM((width, width, depth), jnp.bfloat16),
                pltpu.VMEM((rows, width, depth), jnp.bfloat16),
                pltpu.VMEM((chunk, GROUP * width, width), jnp.bfloat16),
                pltpu.SemaphoreType.DMA((width // GROUP + 1,)),
            ],
        ),
        compiler_params=pltpu.CompilerParams(vmem_limit_bytes=56 << 20),
        cost_estimate=pl.CostEstimate(
            flops=2 * rows * width * size * (depth + pairs),
            bytes_accessed=2 * width * width * depth,
            transcendentals=0,
        ),
    )(start, cholesky, weights)


def sent(sums, after=None):
    sums = jnp.swapaxes(sums, 0, 1).astype(jnp.bfloat16)
    if after is not None:
        sums, after = lax.optimization_barrier((sums, after))
    return lax.all_to_all(sums, BOTH, split_axis=0, concat_axis=0, tiled=True), after


def collected(landed):
    count_i, count_j = lax.axis_size("pi"), lax.axis_size("pj")
    landed = landed.reshape((count_i, count_j, -1) + landed.shape[1:]).astype(jnp.float32)
    return jnp.sum(landed, axis=1)


def shards(amplitudes, cholesky, other_terms):
    width = cholesky.shape[0]
    pair_i, pair_j = amplitudes.shape[:2]
    count_i, count_j = lax.axis_size("pi"), lax.axis_size("pj")
    devices = count_i * count_j
    assert pair_j == 1 and pair_i * count_i == count_j
    rows = width // count_i
    early = rows - rows // 4 if rows % 32 == 0 else rows // 2
    start = lax.axis_index("pi") * rows
    own = packed(amplitudes.reshape(pair_i, width, width))
    copies = jnp.broadcast_to(own[None], (devices,) + own.shape).reshape(devices * pair_i, -1)
    weights = lax.all_to_all(copies, BOTH, split_axis=0, concat_axis=0, tiled=True)
    tile = tiles(cholesky, start.reshape(1), early)
    sums = applied(tile, weights)
    first, _ = sent(sums)
    sums = ladder(cholesky, weights, (start + early).reshape(1), rows - early)
    second, first = sent(sums, first)
    part = jnp.concatenate([collected(first), collected(second)], axis=2)
    part = jnp.swapaxes(part, 0, 1).reshape(pair_i, width, width)
    half = other_terms.reshape(pair_i, width, width) + 0.5 * part
    back = mirrored(half.astype(jnp.bfloat16))
    total = half + jnp.swapaxes(back, 1, 2).astype(jnp.float32)
    return total.reshape(other_terms.shape)


def solution(mesh):
    return jax.shard_map(
        shards,
        mesh=mesh,
        in_specs=(P("pi", "pj", None, None), P(None, None, "pj"), P("pi", "pj", None, None)),
        out_specs=P("pi", "pj", None, None),
        check_vma=False,
    )
```

time: 1060 us -> 143 us (0.13)
  the two profiles are of different devices: /device:TPU:0 before, /device:TPU:3 now
where the time goes in v1:
time: 143 us; the launch traced here: 142 us
  Pallas kernels  83.7 us (59%)
  starting transfers between devices  30.4 us (21%)
  waiting for transfers between devices  15.9 us (11%)
  local copies, waits for them, and re-layouts  8.01 us (6%)
  other arithmetic  3.98 us (3%)
    pallas_call x1, Pallas kernels, tiles(): pl.pallas_call(functools.partial(tile_kernel, rows, chunk), out_shape=jax...  42.3 us
    pallas_call x1, Pallas kernels, applied(): pl.pallas_call(apply_kernel, out_shape=jax.ShapeDtypeStruct((rows, pairs,...  23 us
    pallas_call x1, Pallas kernels, ladder(): pl.pallas_call(functools.partial(ladder_kernel, rows, chunk), out_shape=j...  18.4 us
    ppermute x4, starting transfers between devices, mirrored(): arrived.append(lax.ppermute(sent, BOTH, route))  14.3 us
    all_to_all x2, starting transfers between devices, sent(): lax.all_to_all(sums, BOTH, split_axis=0, concat_axis=0, tiled=True)  13.3 us
    ppermute x4, waiting for transfers between devices, mirrored(): arrived.append(lax.ppermute(sent, BOTH, route))  9.42 us
    all_to_all x2, waiting for transfers between devices, sent(): lax.all_to_all(sums, BOTH, split_axis=0, concat_axis=0, tiled=True)  6.48 us
  transfers between devices with their start and end apart: 7, of which 5 were waited for; matrix products, arithmetic and copies ran while one was open for 1% of the time, Pallas kernels for 43%

profile of v1, /device:TPU:3, one launch (start us, length us, event | category | flops | bytes accessed | tf_op | source)
XLA Modules:
  0.0 142.3 jit_solution(11894950164371979808)
XLA Ops:
  0.0 0.8 constant_dynamic-slice_fusion.2
  0.8 0.1 copy.36
  0.9 5.8 %collective-permute-start = (bf16[128,128]{0,1:T(8,128)(2,1)S(1)}, bf16[128,128]{0,1:T(8,128)(2,1)S(1)}, u32[]{:S(2)}, u32[]{:S(2)}) collective-permute-start(bf16[128,128]{0,1:T(8,128)(2,1)S(1)} %bitcast.57), channel_id=1, source_target_pairs={{0,0},{1,1},{2,8},{3,9},{4,16},{5,17},{6,24},{7,25},{8,2},{9,3},{1... | collective-permute-start | bytes 98312 | tf_op jit(solution)/shard_map/ppermute | solution.py:31
  6.7 0.1 copy.37
  6.8 1.6 %collective-permute-start.1 = (bf16[128,128]{0,1:T(8,128)(2,1)S(1)}, bf16[128,128]{0,1:T(8,128)(2,1)S(1)}, u32[]{:S(2)}, u32[]{:S(2)}) collective-permute-start(bf16[128,128]{0,1:T(8,128)(2,1)S(1)} %bitcast.58), channel_id=1, source_target_pairs={{0,1},{1,0},{2,9},{3,8},{4,17},{5,16},{6,25},{7,24},{8,3},{9,2},{1... | collective-permute-start | bytes 98312 | tf_op jit(solution)/shard_map/ppermute | solution.py:31
  8.4 0.4 collective-permute-done
  8.8 4.9 %collective-permute-done.1 = bf16[128,128]{0,1:T(8,128)(2,1)S(1)} collective-permute-done((bf16[128,128]{0,1:T(8,128)(2,1)S(1)}, bf16[128,128]{0,1:T(8,128)(2,1)S(1)}, u32[]{:S(2)}, u32[]{:S(2)}) %collective-permute-start.1) | collective-permute-done | bytes 32800 | tf_op jit(solution)/shard_map/ppermute | solution.py:31
  13.8 0.9 fusion.3
  14.7 0.1 slice.33
  14.8 0.1 slice.34
  14.9 0.1 slice.35
  14.9 0.1 slice.36
  15.0 0.1 slice.37
  15.1 0.1 slice.38
  15.2 0.1 slice.39
  15.3 0.1 copy.38
  15.4 0.1 reshape.71
  15.5 0.1 copy.39
  15.6 0.1 reshape.72
  15.6 0.1 copy.40
  15.7 0.1 reshape.73
  15.8 0.1 copy.41
  15.9 0.1 reshape.74
  16.0 0.1 copy.42
  16.1 0.1 reshape.75
  16.3 0.1 reshape.76
  16.4 0.1 copy.44
  16.5 0.1 reshape.77
  16.8 1.7 %broadcast_in_dim.22 = bf16[32,2,9216]{2,1,0:T(2,128)(2,1)} broadcast(bf16[2,9216]{1,0:T(2,128)(2,1)S(1)} %constant_dynamic-update-slice_fusion), dimensions={1,2} | broadcast | bytes 1216512 | tf_op jit(solution)/shard_map/broadcast_in_dim | solution.py:258
  18.4 2.8 %all-to-all-start = ((bf16[32,2,9216]{2,1,0:T(2,128)(2,1)}), bf16[32,2,9216]{2,1,0:T(2,128)(2,1)S(1)}, u32[]{:S(2)}, u32[]{:S(2)}) async-start(bf16[32,2,9216]{2,1,0:T(2,128)(2,1)} %broadcast_in_dim.22), calls=%async_computation | async-start | bytes 2359296 | tf_op jit(solution)/shard_map/all_to_all | solution.py:259
  21.2 42.3 %shard_map.38.t_ref = bf16[24,9216,128]{2,1,0:T(8,128)(2,1)} custom-call(s32[1]{0:T(128)} %bitcast.9.start_ref, bf16[128,128,512]{2,1,0:T(8,128)(2,1)} %l_hbm.3), custom_call_target="tpu_custom_call" | custom-call | flops 28991029248 | bytes 73400320 | tf_op jit(solution)/shard_map/pallas_call | solution.py:126
  63.6 1.3 all_to_all.12.s_ref
  64.8 23.0 %shard_map.39 = f32[24,64,128]{2,1,0:T(8,128)} custom-call(bf16[24,9216,128]{2,1,0:T(8,128)(2,1)} %shard_map.38.t_ref, bf16[64,9216]{1,0:T(8,128)(2,1)} %all_to_all.12.s_ref), custom_call_target="tpu_custom_call" | custom-call | flops 3623878656 | bytes 56623104 | tf_op jit(solution)/shard_map/pallas_call | solution.py:160
  87.9 1.2 convert_bitcast_fusion
  89.1 1.0 copy.46
  90.1 7.4 %all-to-all-start.1 = ((bf16[64,24,128]{2,1,0:T(8,128)(2,1)}), bf16[64,24,128]{2,1,0:T(8,128)(2,1)S(1)}, u32[]{:S(2)}, u32[]{:S(2)}) async-start(bf16[64,24,128]{2,1,0:T(8,128)(2,1)} %copy.46), calls=%async_computation.1 | async-start | bytes 786432 | tf_op jit(solution)/shard_map/all_to_all | solution.py:239
  97.5 18.4 %shard_map.37 = f32[8,64,128]{2,1,0:T(8,128)} custom-call(s32[1]{0:T(128)} %bitcast.1.start_ref, bf16[128,128,512]{2,1,0:T(8,128)(2,1)} %l_hbm.3, bf16[64,9216]{1,0:T(8,128)(2,1)} %all_to_all.12.s_ref), custom_call_target="tpu_custom_call" | custom-call | flops 10871635968 | bytes 16777216 | tf_op jit(solution)/shard_map/pallas_call | solution.py:211
  115.9 1.0 convert_bitcast_fusion.2
  116.9 0.7 copy.48
  117.7 5.8 %all-to-all-start.2 = ((bf16[64,8,128]{2,1,0:T(8,128)(2,1)}), bf16[64,8,128]{2,1,0:T(8,128)(2,1)S(1)}, u32[]{:S(2)}, u32[]{:S(2)}) async-start(bf16[64,8,128]{2,1,0:T(8,128)(2,1)} %copy.48), calls=%async_computation.2 | async-start | bytes 262144 | tf_op jit(solution)/shard_map/all_to_all | solution.py:239
  123.6 6.5 %all-to-all-done.2 = bf16[64,8,128]{2,1,0:T(8,128)(2,1)S(1)} async-done(((bf16[64,8,128]{2,1,0:T(8,128)(2,1)}), bf16[64,8,128]{2,1,0:T(8,128)(2,1)S(1)}, u32[]{:S(2)}, u32[]{:S(2)}) %all-to-all-start.2) | async-done | bytes 131104 | tf_op jit(solution)/shard_map/all_to_all | solution.py:239
  130.3 0.1 copy.51
  130.5 4.1 %collective-permute-start.2 = (bf16[128,128]{0,1:T(8,128)(2,1)S(1)}, bf16[128,128]{0,1:T(8,128)(2,1)S(1)}, u32[]{:S(2)}, u32[]{:S(2)}) collective-permute-start(bf16[128,128]{0,1:T(8,128)(2,1)S(1)} %bitcast.59), channel_id=1, source_target_pairs={{0,0},{1,1},{2,8},{3,9},{4,16},{5,17},{6,24},{7,25},{8,2},{9,3},{1... | collective-permute-start | bytes 98312 | tf_op jit(solution)/shard_map/ppermute | solution.py:31
  134.5 0.1 copy.52
  134.6 2.9 %collective-permute-start.3 = (bf16[128,128]{0,1:T(8,128)(2,1)S(1)}, bf16[128,128]{0,1:T(8,128)(2,1)S(1)}, u32[]{:S(2)}, u32[]{:S(2)}) collective-permute-start(bf16[128,128]{0,1:T(8,128)(2,1)S(1)} %bitcast.60), channel_id=1, source_target_pairs={{0,1},{1,0},{2,9},{3,8},{4,17},{5,16},{6,25},{7,24},{8,3},{9,2},{1... | collective-permute-start | bytes 98312 | tf_op jit(solution)/shard_map/ppermute | solution.py:31
  137.6 1.0 collective-permute-done.2
  138.5 3.1 %collective-permute-done.3 = bf16[128,128]{0,1:T(8,128)(2,1)S(1)} collective-permute-done((bf16[128,128]{0,1:T(8,128)(2,1)S(1)}, bf16[128,128]{0,1:T(8,128)(2,1)S(1)}, u32[]{:S(2)}, u32[]{:S(2)}) %collective-permute-start.3) | collective-permute-done | bytes 32800 | tf_op jit(solution)/shard_map/ppermute | solution.py:31
  141.7 0.7 fusion.4
  (26 shorter events, 0.6 us)
Async XLA Ops:
  0.9 7.9 %collective-permute-start = (bf16[128,128]{0,1:T(8,128)(2,1)S(1)}, bf16[128,128]{0,1:T(8,128)(2,1)S(1)}, u32[]{:S(2)}, u32[]{:S(2)}) collective-permute-start(bf16[128,128]{0,1:T(8,128)(2,1)S(1)} %bitcast.57), channel_id=1, source_target_pairs={{0,0},{1,1},{2,8},{3,9},{4,16},{5,17},{6,24},{7,25},{8,2},{9,3},{1... | collective-permute-start | bytes 98312 | tf_op jit(solution)/shard_map/ppermute | solution.py:31
  6.8 7.0 %collective-permute-start.1 = (bf16[128,128]{0,1:T(8,128)(2,1)S(1)}, bf16[128,128]{0,1:T(8,128)(2,1)S(1)}, u32[]{:S(2)}, u32[]{:S(2)}) collective-permute-start(bf16[128,128]{0,1:T(8,128)(2,1)S(1)} %bitcast.58), channel_id=1, source_target_pairs={{0,1},{1,0},{2,9},{3,8},{4,17},{5,16},{6,25},{7,24},{8,3},{9,2},{1... | collective-permute-start | bytes 98312 | tf_op jit(solution)/shard_map/ppermute | solution.py:31
  18.4 45.1 %all-to-all-start = ((bf16[32,2,9216]{2,1,0:T(2,128)(2,1)}), bf16[32,2,9216]{2,1,0:T(2,128)(2,1)S(1)}, u32[]{:S(2)}, u32[]{:S(2)}) async-start(bf16[32,2,9216]{2,1,0:T(2,128)(2,1)} %broadcast_in_dim.22), calls=%async_computation | async-start | bytes 2359296 | tf_op jit(solution)/shard_map/all_to_all | solution.py:259
  90.1 26.9 %all-to-all-start.1 = ((bf16[64,24,128]{2,1,0:T(8,128)(2,1)}), bf16[64,24,128]{2,1,0:T(8,128)(2,1)S(1)}, u32[]{:S(2)}, u32[]{:S(2)}) async-start(bf16[64,24,128]{2,1,0:T(8,128)(2,1)} %copy.46), calls=%async_computation.1 | async-start | bytes 786432 | tf_op jit(solution)/shard_map/all_to_all | solution.py:239
  115.9 14.4 %copy-start = (f32[2,1,128,128]{3,2,1,0:T(8,128)S(1)}, f32[2,1,128,128]{3,2,1,0:T(8,128)}, u32[]{:S(2)}) copy-start(f32[2,1,128,128]{3,2,1,0:T(8,128)} %param.5) | copy-start | bytes 393220
  117.7 12.4 %all-to-all-start.2 = ((bf16[64,8,128]{2,1,0:T(8,128)(2,1)}), bf16[64,8,128]{2,1,0:T(8,128)(2,1)S(1)}, u32[]{:S(2)}, u32[]{:S(2)}) async-start(bf16[64,8,128]{2,1,0:T(8,128)(2,1)} %copy.48), calls=%async_computation.2 | async-start | bytes 262144 | tf_op jit(solution)/shard_map/all_to_all | solution.py:239
  130.5 8.1 %collective-permute-start.2 = (bf16[128,128]{0,1:T(8,128)(2,1)S(1)}, bf16[128,128]{0,1:T(8,128)(2,1)S(1)}, u32[]{:S(2)}, u32[]{:S(2)}) collective-permute-start(bf16[128,128]{0,1:T(8,128)(2,1)S(1)} %bitcast.59), channel_id=1, source_target_pairs={{0,0},{1,1},{2,8},{3,9},{4,16},{5,17},{6,24},{7,25},{8,2},{9,3},{1... | collective-permute-start | bytes 98312 | tf_op jit(solution)/shard_map/ppermute | solution.py:31
  134.6 7.0 %collective-permute-start.3 = (bf16[128,128]{0,1:T(8,128)(2,1)S(1)}, bf16[128,128]{0,1:T(8,128)(2,1)S(1)}, u32[]{:S(2)}, u32[]{:S(2)}) collective-permute-start(bf16[128,128]{0,1:T(8,128)(2,1)S(1)} %bitcast.60), channel_id=1, source_target_pairs={{0,1},{1,0},{2,9},{3,8},{4,17},{5,16},{6,25},{7,24},{8,3},{9,2},{1... | collective-permute-start | bytes 98312 | tf_op jit(solution)/shard_map/ppermute | solution.py:31

commit v2 on v1

--- a/solution.py
+++ b/solution.py
@@ -139,7 +139,7 @@
                 pltpu.SemaphoreType.DMA((2,)),
             ],
         ),
-        compiler_params=pltpu.CompilerParams(vmem_limit_bytes=56 << 20),
+        compiler_params=pltpu.CompilerParams(vmem_limit_bytes=60 << 20),
         cost_estimate=pl.CostEstimate(
             flops=2 * rows * width * size * depth,
             bytes_accessed=2 * width * width * depth + 2 * rows * size * width,
@@ -148,35 +148,22 @@
     )(start, cholesky)
 
 
-def apply_kernel(t_ref, s_ref, out_ref):
-    for a in range(t_ref.shape[0]):
-        out_ref[a] = lax.dot_general(s_ref[...], t_ref[a], NN, preferred_element_type=jnp.float32)
-
-
-def applied(tile, weights):
-    rows, size, width = tile.shape
-    pairs = weights.shape[0]
-    each = 2 if rows % 2 == 0 else 1
-    return pl.pallas_call(
-        apply_kernel,
-        out_shape=jax.ShapeDtypeStruct((rows, pairs, width), jnp.float32),
-        grid=(rows // each,),
-        in_specs=[pl.BlockSpec((each, size, width), lambda a: (a, 0, 0)), VMEM],
-        out_specs=pl.BlockSpec((each, pairs, width), lambda a: (a, 0, 0)),
-        compiler_params=pltpu.CompilerParams(vmem_limit_bytes=56 << 20),
-        cost_estimate=pl.CostEstimate(
-            flops=2 * rows * width * size * pairs,
-            bytes_accessed=2 * rows * size * width,
-            transcendentals=0,
-        ),
-    )(tile, weights)
-
-
-def ladder_kernel(rows, chunk, start_ref, l_hbm, s_ref, out_ref, vectors, own, tile, sems):
+def ladder_kernel(
+    early, chunk, start_ref, l_hbm, t_hbm, s_ref, out_ref, vectors, own, tile, ring, total, sems, got
+):
     width = vectors.shape[0]
     blocks = width // GROUP
+    late = own.shape[0]
+    slots = ring.shape[0]
     at_row = offsets(width)
-    copies = load(start_ref[0], rows, l_hbm, own, vectors, sems)
+    copies = load(start_ref[0] + early, late, l_hbm, own, vectors, sems)
+
+    def fetch(a):
+        slot = lax.rem(a, slots)
+        return pltpu.make_async_copy(t_hbm.at[a], ring.at[slot], got.at[slot])
+
+    for a in range(slots):
+        fetch(a).start()
     copies[0].wait()
 
     def step(at, carry):
@@ -196,51 +183,62 @@
                     preferred_element_type=jnp.float32,
                 )
                 if k == 0:
-                    out_ref[at * chunk + a] = value
+                    total[early + at * chunk + a] = value
                 else:
-                    out_ref[at * chunk + a] += value
+                    total[early + at * chunk + a] += value
         return carry
 
-    lax.fori_loop(0, rows // chunk, step, 0)
-
-
-def ladder(cholesky, weights, start, rows):
+    lax.fori_loop(0, late // chunk, step, 0)
+
+    def rest(a, carry):
+        fetch(a).wait()
+        total[a] = lax.dot_general(
+            s_ref[...], ring[lax.rem(a, slots)], NN, preferred_element_type=jnp.float32
+        )
+        pl.when(a + slots < early)(lambda: fetch(a + slots).start())
+        return carry
+
+    lax.fori_loop(0, early, rest, 0)
+    out_ref[...] = jnp.swapaxes(total[...], 0, 1).astype(out_ref.dtype)
+
+
+def ladder(cholesky, tile, weights, start, rows):
     width, _, depth = cholesky.shape
+    early = tile.shape[0]
+    late = rows - early
     pairs, size = weights.shape
-    chunk = min(8, rows)
+    chunk = min(8, late)
+    slots = min(early, 10)
     return pl.pallas_call(
-        functools.partial(ladder_kernel, rows, chunk),
-        out_shape=jax.ShapeDtypeStruct((rows, pairs, width), jnp.float32),
+        functools.partial(ladder_kernel, early, chunk),
+        out_shape=jax.ShapeDtypeStruct((pairs, rows, width), jnp.bfloat16),
         grid_spec=pltpu.PrefetchScalarGridSpec(
             num_scalar_prefetch=1,
             grid=(),
-            in_specs=[ANY, VMEM],
+            in_specs=[ANY, ANY, VMEM],
             out_specs=VMEM,
             scratch_shapes=[
                 pltpu.VMEM((width, width, depth), jnp.bfloat16),
-                pltpu.VMEM((rows, width, depth), jnp.bfloat16),
+                pltpu.VMEM((late, width, depth), jnp.bfloat16),
                 pltpu.VMEM((chunk, GROUP * width, width), jnp.bfloat16),
+                pltpu.VMEM((slots, size, width), jnp.bfloat16),
+                pltpu.VMEM((rows, pairs, width), jnp.float32),
                 pltpu.SemaphoreType.DMA((width // GROUP + 1,)),
+                pltpu.SemaphoreType.DMA((slots,)),
             ],
         ),
-        compiler_params=pltpu.CompilerParams(vmem_limit_bytes=56 << 20),
+        compiler_params=pltpu.CompilerParams(vmem_limit_bytes=62 << 20),
         cost_estimate=pl.CostEstimate(
-            flops=2 * rows * width * size * (depth + pairs),
-            bytes_accessed=2 * width * width * depth,
+            flops=2 * width * size * (late * depth + rows * pairs),
+            bytes_accessed=2 * width * width * depth + 2 * early * size * width,
             transcendentals=0,
         ),
-    )(start, cholesky, weights)
-
-
-def sent(sums, after=None):
-    sums = jnp.swapaxes(sums, 0, 1).astype(jnp.bfloat16)
-    if after is not None:
-        sums, after = lax.optimization_barrier((sums, after))
-    return lax.all_to_all(sums, BOTH, split_axis=0, concat_axis=0, tiled=True), after
-
-
-def collected(landed):
+    )(start, cholesky, tile, weights)
+
+
+def collected(sums):
     count_i, count_j = lax.axis_size("pi"), lax.axis_size("pj")
+    landed = lax.all_to_all(sums, BOTH, split_axis=0, concat_axis=0, tiled=True)
     landed = landed.reshape((count_i, count_j, -1) + landed.shape[1:]).astype(jnp.float32)
     return jnp.sum(landed, axis=1)
 
@@ -252,17 +250,13 @@
     devices = count_i * count_j
     assert pair_j == 1 and pair_i * count_i == count_j
     rows = width // count_i
-    early = rows - rows // 4 if rows % 32 == 0 else rows // 2
-    start = lax.axis_index("pi") * rows
+    early = rows // 2
+    start = (lax.axis_index("pi") * rows).reshape(1)
     own = packed(amplitudes.reshape(pair_i, width, width))
     copies = jnp.broadcast_to(own[None], (devices,) + own.shape).reshape(devices * pair_i, -1)
     weights = lax.all_to_all(copies, BOTH, split_axis=0, concat_axis=0, tiled=True)
-    tile = tiles(cholesky, start.reshape(1), early)
-    sums = applied(tile, weights)
-    first, _ = sent(sums)
-    sums = ladder(cholesky, weights, (start + early).reshape(1), rows - early)
-    second, first = sent(sums, first)
-    part = jnp.concatenate([collected(first), collected(second)], axis=2)
+    tile = tiles(cholesky, start, early)
+    part = collected(ladder(cholesky, tile, weights, start, rows))
     part = jnp.swapaxes(part, 0, 1).reshape(pair_i, width, width)
     half = other_terms.reshape(pair_i, width, width) + 0.5 * part
     back = mirrored(half.astype(jnp.bfloat16))

time: 143 us -> 135 us (0.944)
  blocking collectives: 0 us -> 27.4 us
  starting transfers between devices: 30.4 us -> 16.7 us
  Pallas kernels: 83.7 us -> 72.8 us
  waiting for transfers between devices: 15.9 us -> 9.58 us
  other arithmetic: 3.98 us -> 1.73 us
  local copies, waits for them, and re-layouts: 8.01 us -> 6.19 us
    all_to_all x0 -> x1, blocking collectives: none -> 27.4 us  [collected(): landed = lax.all_to_all(sums, BOTH, split_axis=0, concat_axis=0, tiled=True)]
    all_to_all x2 -> x0, starting transfers between devices: 13.3 us -> none  [sent(): lax.all_to_all(sums, BOTH, split_axis=0, concat_axis=0, tiled=True)]
    pallas_call x1, Pallas kernels: 42.3 us -> 29.2 us  [tiles(): pl.pallas_call(functools.partial(tile_kernel, rows, chunk), out_shape=jax...]
    all_to_all x2 -> x0, waiting for transfers between devices: 6.48 us -> none  [sent(): lax.all_to_all(sums, BOTH, split_axis=0, concat_axis=0, tiled=True)]
    convert_element_type x2 -> x0, other arithmetic: 2.2 us -> none  [sent(): sums = jnp.swapaxes(sums, 0, 1).astype(jnp.bfloat16)]
    pallas_call x2 -> x1, Pallas kernels: 41.4 us -> 43.6 us  [ladder(): pl.pallas_call(functools.partial(ladder_kernel, early, chunk), out_shape=...]
  transfers between devices with their start and end apart: 7 -> 5, of which waited for: 5 -> 5; matrix products, arithmetic and copies ran while one was open for 1% -> 0% of each run, Pallas kernels for 43% -> 22%
where the time goes in v2:
time: 135 us
  Pallas kernels  72.8 us (54%)
  blocking collectives  27.4 us (20%)
  starting transfers between devices  16.7 us (12%)
  waiting for transfers between devices  9.58 us (7%)
  local copies, waits for them, and re-layouts  6.19 us (5%)
  other arithmetic  1.73 us (1%)
    pallas_call x1, Pallas kernels, ladder(): pl.pallas_call(functools.partial(ladder_kernel, early, chunk), out_shape=...  43.6 us
    pallas_call x1, Pallas kernels, tiles(): pl.pallas_call(functools.partial(tile_kernel, rows, chunk), out_shape=jax...  29.2 us
    all_to_all x1, blocking collectives, collected(): landed = lax.all_to_all(sums, BOTH, split_axis=0, concat_axis=0, tiled=True)  27.4 us
    ppermute x4, starting transfers between devices, mirrored(): arrived.append(lax.ppermute(sent, BOTH, route))  13.9 us
    ppermute x4, waiting for transfers between devices, mirrored(): arrived.append(lax.ppermute(sent, BOTH, route))  9.47 us
    all_to_all x1, starting transfers between devices, shards(): lax.all_to_all(copies, BOTH, split_axis=0, concat_axis=0, tiled=True)  2.81 us
  transfers between devices with their start and end apart: 5, of which 5 were waited for; matrix products, arithmetic and copies ran while one was open for 0% of the time, Pallas kernels for 22%

profile of v2, /device:TPU:3, one launch (start us, length us, event | category | flops | bytes accessed | tf_op | source)
XLA Modules:
  0.0 134.6 jit_solution(473367011212211960)
XLA Ops:
  0.0 0.8 constant_dynamic-slice_fusion.2
  0.8 0.1 copy.32
  0.9 5.8 %collective-permute-start = (bf16[128,128]{0,1:T(8,128)(2,1)S(1)}, bf16[128,128]{0,1:T(8,128)(2,1)S(1)}, u32[]{:S(2)}, u32[]{:S(2)}) collective-permute-start(bf16[128,128]{0,1:T(8,128)(2,1)S(1)} %bitcast.49), channel_id=1, source_target_pairs={{0,0},{1,1},{2,8},{3,9},{4,16},{5,17},{6,24},{7,25},{8,2},{9,3},{1... | collective-permute-start | bytes 98312 | tf_op jit(solution)/shard_map/ppermute | solution.py:31
  6.7 0.1 copy.33
  6.8 1.6 %collective-permute-start.1 = (bf16[128,128]{0,1:T(8,128)(2,1)S(1)}, bf16[128,128]{0,1:T(8,128)(2,1)S(1)}, u32[]{:S(2)}, u32[]{:S(2)}) collective-permute-start(bf16[128,128]{0,1:T(8,128)(2,1)S(1)} %bitcast.50), channel_id=1, source_target_pairs={{0,1},{1,0},{2,9},{3,8},{4,17},{5,16},{6,25},{7,24},{8,3},{9,2},{1... | collective-permute-start | bytes 98312 | tf_op jit(solution)/shard_map/ppermute | solution.py:31
  8.4 0.4 collective-permute-done
  8.8 4.9 %collective-permute-done.1 = bf16[128,128]{0,1:T(8,128)(2,1)S(1)} collective-permute-done((bf16[128,128]{0,1:T(8,128)(2,1)S(1)}, bf16[128,128]{0,1:T(8,128)(2,1)S(1)}, u32[]{:S(2)}, u32[]{:S(2)}) %collective-permute-start.1) | collective-permute-done | bytes 32800 | tf_op jit(solution)/shard_map/ppermute | solution.py:31
  13.8 0.9 fusion.2
  14.7 0.1 slice.33
  14.8 0.1 slice.34
  14.9 0.1 slice.35
  14.9 0.1 slice.36
  15.0 0.1 slice.37
  15.1 0.1 slice.38
  15.2 0.1 slice.39
  15.3 0.1 copy.34
  15.4 0.1 reshape.65
  15.5 0.1 copy.35
  15.5 0.1 reshape.66
  15.6 0.1 copy.36
  15.7 0.1 reshape.67
  15.8 0.1 copy.37
  15.9 0.1 reshape.68
  16.0 0.1 copy.38
  16.1 0.1 reshape.69
  16.2 0.1 copy.39
  16.3 0.1 reshape.70
  16.4 0.1 copy.40
  16.4 0.1 reshape.71
  16.6 0.1 copy.41
  16.8 1.6 %broadcast_in_dim.22 = bf16[32,2,9216]{2,1,0:T(2,128)(2,1)} broadcast(bf16[2,9216]{1,0:T(2,128)(2,1)S(1)} %constant_dynamic-update-slice_fusion), dimensions={1,2} | broadcast | bytes 1216512 | tf_op jit(solution)/shard_map/broadcast_in_dim | solution.py:256
  18.4 2.8 %all-to-all-start = ((bf16[32,2,9216]{2,1,0:T(2,128)(2,1)}), bf16[32,2,9216]{2,1,0:T(2,128)(2,1)S(1)}, u32[]{:S(2)}, u32[]{:S(2)}) async-start(bf16[32,2,9216]{2,1,0:T(2,128)(2,1)} %broadcast_in_dim.22), calls=%async_computation | async-start | bytes 2359296 | tf_op jit(solution)/shard_map/all_to_all | solution.py:257
  21.2 29.2 %shard_map.37.t_hbm = bf16[16,9216,128]{2,1,0:T(8,128)(2,1)} custom-call(s32[1]{0:T(128)} %bitcast.1.start_ref, bf16[128,128,512]{2,1,0:T(8,128)(2,1)} %l_hbm.3), custom_call_target="tpu_custom_call" | custom-call | flops 19327352832 | bytes 54525952 | tf_op jit(solution)/shard_map/pallas_call | solution.py:126
  50.5 0.1 all-to-all-done
  50.6 1.3 all_to_all.9.s_ref
  51.9 43.6 %shard_map.38 = bf16[64,32,128]{2,1,0:T(8,128)(2,1)} custom-call(s32[1]{0:T(128)} %bitcast.1.start_ref, bf16[128,128,512]{2,1,0:T(8,128)(2,1)} %l_hbm.3, bf16[16,9216,128]{2,1,0:T(8,128)(2,1)} %shard_map.37.t_hbm, bf16[64,9216]{1,0:T(8,128)(2,1)} %all_to_all.9.s_ref), custom_call_target="tpu_custom_call" | custom-call | flops 24159191040 | bytes 54525952 | tf_op jit(solution)/shard_map/pallas_call | solution.py:212
  95.5 0.0 copy-start
  95.5 27.4 %all_to_all.13 = bf16[64,32,128]{2,1,0:T(8,128)(2,1)S(1)} all-to-all(bf16[64,32,128]{2,1,0:T(8,128)(2,1)} %shard_map.38), channel_id=1, replica_groups=mesh['pi'=4,'pj'=8] {'pi','pj'}, dimensions={0} | all-to-all | bytes 1048576 | tf_op jit(solution)/shard_map/all_to_all | solution.py:241
  122.8 0.1 convert_reduce_fusion
  123.0 0.0 copy-done
  123.0 0.1 copy.44
  123.1 0.1 copy.43
  123.3 3.6 %collective-permute-start.2 = (bf16[128,128]{0,1:T(8,128)(2,1)S(1)}, bf16[128,128]{0,1:T(8,128)(2,1)S(1)}, u32[]{:S(2)}, u32[]{:S(2)}) collective-permute-start(bf16[128,128]{0,1:T(8,128)(2,1)S(1)} %bitcast.52), channel_id=1, source_target_pairs={{0,0},{1,1},{2,8},{3,9},{4,16},{5,17},{6,24},{7,25},{8,2},{9,3},{1... | collective-permute-start | bytes 98312 | tf_op jit(solution)/shard_map/ppermute | solution.py:31
  126.9 2.9 %collective-permute-start.3 = (bf16[128,128]{0,1:T(8,128)(2,1)S(1)}, bf16[128,128]{0,1:T(8,128)(2,1)S(1)}, u32[]{:S(2)}, u32[]{:S(2)}) collective-permute-start(bf16[128,128]{0,1:T(8,128)(2,1)S(1)} %bitcast.51), channel_id=1, source_target_pairs={{0,1},{1,0},{2,9},{3,8},{4,17},{5,16},{6,25},{7,24},{8,3},{9,2},{1... | collective-permute-start | bytes 98312 | tf_op jit(solution)/shard_map/ppermute | solution.py:31
  129.8 2.0 %collective-permute-done.2 = bf16[128,128]{0,1:T(8,128)(2,1)S(1)} collective-permute-done((bf16[128,128]{0,1:T(8,128)(2,1)S(1)}, bf16[128,128]{0,1:T(8,128)(2,1)S(1)}, u32[]{:S(2)}, u32[]{:S(2)}) %collective-permute-start.2) | collective-permute-done | bytes 32800 | tf_op jit(solution)/shard_map/ppermute | solution.py:31
  131.8 2.1 %collective-permute-done.3 = bf16[128,128]{0,1:T(8,128)(2,1)S(1)} collective-permute-done((bf16[128,128]{0,1:T(8,128)(2,1)S(1)}, bf16[128,128]{0,1:T(8,128)(2,1)S(1)}, u32[]{:S(2)}, u32[]{:S(2)}) %collective-permute-start.3) | collective-permute-done | bytes 32800 | tf_op jit(solution)/shard_map/ppermute | solution.py:31
  133.9 0.7 fusion.3
  (16 shorter events, 0.2 us)
Async XLA Ops:
  0.9 7.9 %collective-permute-start = (bf16[128,128]{0,1:T(8,128)(2,1)S(1)}, bf16[128,128]{0,1:T(8,128)(2,1)S(1)}, u32[]{:S(2)}, u32[]{:S(2)}) collective-permute-start(bf16[128,128]{0,1:T(8,128)(2,1)S(1)} %bitcast.49), channel_id=1, source_target_pairs={{0,0},{1,1},{2,8},{3,9},{4,16},{5,17},{6,24},{7,25},{8,2},{9,3},{1... | collective-permute-start | bytes 98312 | tf_op jit(solution)/shard_map/ppermute | solution.py:31
  6.8 7.0 %collective-permute-start.1 = (bf16[128,128]{0,1:T(8,128)(2,1)S(1)}, bf16[128,128]{0,1:T(8,128)(2,1)S(1)}, u32[]{:S(2)}, u32[]{:S(2)}) collective-permute-start(bf16[128,128]{0,1:T(8,128)(2,1)S(1)} %bitcast.50), channel_id=1, source_target_pairs={{0,1},{1,0},{2,9},{3,8},{4,17},{5,16},{6,25},{7,24},{8,3},{9,2},{1... | collective-permute-start | bytes 98312 | tf_op jit(solution)/shard_map/ppermute | solution.py:31
  18.4 32.2 %all-to-all-start = ((bf16[32,2,9216]{2,1,0:T(2,128)(2,1)}), bf16[32,2,9216]{2,1,0:T(2,128)(2,1)S(1)}, u32[]{:S(2)}, u32[]{:S(2)}) async-start(bf16[32,2,9216]{2,1,0:T(2,128)(2,1)} %broadcast_in_dim.22), calls=%async_computation | async-start | bytes 2359296 | tf_op jit(solution)/shard_map/all_to_all | solution.py:257
  95.5 27.5 %copy-start = (f32[2,1,128,128]{3,2,1,0:T(8,128)S(1)}, f32[2,1,128,128]{3,2,1,0:T(8,128)}, u32[]{:S(2)}) copy-start(f32[2,1,128,128]{3,2,1,0:T(8,128)} %param.5) | copy-start | bytes 393220
  123.3 8.5 %collective-permute-start.2 = (bf16[128,128]{0,1:T(8,128)(2,1)S(1)}, bf16[128,128]{0,1:T(8,128)(2,1)S(1)}, u32[]{:S(2)}, u32[]{:S(2)}) collective-permute-start(bf16[128,128]{0,1:T(8,128)(2,1)S(1)} %bitcast.52), channel_id=1, source_target_pairs={{0,0},{1,1},{2,8},{3,9},{4,16},{5,17},{6,24},{7,25},{8,2},{9,3},{1... | collective-permute-start | bytes 98312 | tf_op jit(solution)/shard_map/ppermute | solution.py:31
  126.9 7.0 %collective-permute-start.3 = (bf16[128,128]{0,1:T(8,128)(2,1)S(1)}, bf16[128,128]{0,1:T(8,128)(2,1)S(1)}, u32[]{:S(2)}, u32[]{:S(2)}) collective-permute-start(bf16[128,128]{0,1:T(8,128)(2,1)S(1)} %bitcast.51), channel_id=1, source_target_pairs={{0,1},{1,0},{2,9},{3,8},{4,17},{5,16},{6,25},{7,24},{8,3},{9,2},{1... | collective-permute-start | bytes 98312 | tf_op jit(solution)/shard_map/ppermute | solution.py:31

commit v3 on v2

--- a/solution.py
+++ b/solution.py
@@ -59,15 +59,27 @@
     return at
 
 
-def load(start, rows, l_hbm, own, vectors, sems):
+AHEAD = 3
+
+
+def loads(start, rows, l_hbm, own, vectors, sems):
     blocks = vectors.shape[0] // GROUP
     copies = [pltpu.make_async_copy(l_hbm.at[pl.ds(start, rows)], own, sems.at[blocks])]
     for k in range(blocks):
         part = pl.ds(k * GROUP, GROUP)
         copies.append(pltpu.make_async_copy(l_hbm.at[part], vectors.at[part], sems.at[k]))
-    for copy in copies:
+    for copy in copies[: AHEAD + 1]:
         copy.start()
-    return copies
+    copies[0].wait()
+    return copies[1:]
+
+
+def arrive(copies, k, then):
+    copies[k].wait()
+    if k + AHEAD < len(copies):
+        copies[k + AHEAD].start()
+    if k + 1 == len(copies):
+        then()
 
 
 def form(own, vectors, at, chunk, k, store):
@@ -87,8 +99,7 @@
     width = vectors.shape[0]
     blocks = width // GROUP
     at_row = offsets(width)
-    copies = load(start_ref[0], rows, l_hbm, own, vectors, sems)
-    copies[0].wait()
+    copies = loads(start_ref[0], rows, l_hbm, own, vectors, sems)
 
     def out_copy(at, k):
         size = at_row[k + 1] - at_row[k]
@@ -100,7 +111,7 @@
 
     def step(at, carry):
         for k in range(blocks):
-            pl.when(at == 0)(copies[k + 1].wait)
+            pl.when(at == 0)(functools.partial(arrive, copies, k, lambda: None))
             if k >= 2:
                 out_copy(at, k - 2).wait()
             else:
@@ -156,19 +167,19 @@
     late = own.shape[0]
     slots = ring.shape[0]
     at_row = offsets(width)
-    copies = load(start_ref[0] + early, late, l_hbm, own, vectors, sems)
+    copies = loads(start_ref[0] + early, late, l_hbm, own, vectors, sems)
 
     def fetch(a):
         slot = lax.rem(a, slots)
         return pltpu.make_async_copy(t_hbm.at[a], ring.at[slot], got.at[slot])
 
-    for a in range(slots):
-        fetch(a).start()
-    copies[0].wait()
+    def prefetch():
+        for a in range(slots):
+            fetch(a).start()
 
     def step(at, carry):
         for k in range(blocks):
-            pl.when(at == 0)(copies[k + 1].wait)
+            pl.when(at == 0)(functools.partial(arrive, copies, k, prefetch))
 
             def store(part, value):
                 tile[:, part] = value

time: 135 us -> 127 us (0.941)
  blocking collectives: 27.4 us -> 21.5 us
  Pallas kernels: 72.8 us -> 70.8 us
    all_to_all x1, blocking collectives: 27.4 us -> 21.5 us  [collected(): landed = lax.all_to_all(sums, BOTH, split_axis=0, concat_axis=0, tiled=True)]
    pallas_call x1, Pallas kernels: 43.6 us -> 41.6 us  [ladder(): pl.pallas_call(functools.partial(ladder_kernel, early, chunk), out_shape=...]
  transfers between devices with their start and end apart: 5 -> 5, of which waited for: 5 -> 5; matrix products, arithmetic and copies ran while one was open for 0% -> 0% of each run, Pallas kernels for 22% -> 23%
where the time goes in v3:
time: 127 us
  Pallas kernels  70.8 us (56%)
  blocking collectives  21.5 us (17%)
  starting transfers between devices  16.7 us (13%)
  waiting for transfers between devices  9.58 us (8%)
  local copies, waits for them, and re-layouts  6.19 us (5%)
  other arithmetic  1.73 us (1%)
    pallas_call x1, Pallas kernels, ladder(): pl.pallas_call(functools.partial(ladder_kernel, early, chunk), out_shape=...  41.6 us
    pallas_call x1, Pallas kernels, tiles(): pl.pallas_call(functools.partial(tile_kernel, rows, chunk), out_shape=jax...  29.2 us
    all_to_all x1, blocking collectives, collected(): landed = lax.all_to_all(sums, BOTH, split_axis=0, concat_axis=0, tiled=True)  21.5 us
    ppermute x4, starting transfers between devices, mirrored(): arrived.append(lax.ppermute(sent, BOTH, route))  13.9 us
    ppermute x4, waiting for transfers between devices, mirrored(): arrived.append(lax.ppermute(sent, BOTH, route))  9.47 us
    all_to_all x1, starting transfers between devices, shards(): lax.all_to_all(copies, BOTH, split_axis=0, concat_axis=0, tiled=True)  2.81 us
  transfers between devices with their start and end apart: 5, of which 5 were waited for; matrix products, arithmetic and copies ran while one was open for 0% of the time, Pallas kernels for 23%

profile of v3, /device:TPU:3, one launch (start us, length us, event | category | flops | bytes accessed | tf_op | source)
XLA Modules:
  0.0 126.8 jit_solution(11941221823221423067)
XLA Ops:
  0.0 0.8 constant_dynamic-slice_fusion.2
  0.8 0.1 copy.32
  0.9 5.8 %collective-permute-start = (bf16[128,128]{0,1:T(8,128)(2,1)S(1)}, bf16[128,128]{0,1:T(8,128)(2,1)S(1)}, u32[]{:S(2)}, u32[]{:S(2)}) collective-permute-start(bf16[128,128]{0,1:T(8,128)(2,1)S(1)} %bitcast.49), channel_id=1, source_target_pairs={{0,0},{1,1},{2,8},{3,9},{4,16},{5,17},{6,24},{7,25},{8,2},{9,3},{1... | collective-permute-start | bytes 98312 | tf_op jit(solution)/shard_map/ppermute | solution.py:31
  6.7 0.1 copy.33
  6.8 1.6 %collective-permute-start.1 = (bf16[128,128]{0,1:T(8,128)(2,1)S(1)}, bf16[128,128]{0,1:T(8,128)(2,1)S(1)}, u32[]{:S(2)}, u32[]{:S(2)}) collective-permute-start(bf16[128,128]{0,1:T(8,128)(2,1)S(1)} %bitcast.50), channel_id=1, source_target_pairs={{0,1},{1,0},{2,9},{3,8},{4,17},{5,16},{6,25},{7,24},{8,3},{9,2},{1... | collective-permute-start | bytes 98312 | tf_op jit(solution)/shard_map/ppermute | solution.py:31
  8.4 0.4 collective-permute-done
  8.8 4.9 %collective-permute-done.1 = bf16[128,128]{0,1:T(8,128)(2,1)S(1)} collective-permute-done((bf16[128,128]{0,1:T(8,128)(2,1)S(1)}, bf16[128,128]{0,1:T(8,128)(2,1)S(1)}, u32[]{:S(2)}, u32[]{:S(2)}) %collective-permute-start.1) | collective-permute-done | bytes 32800 | tf_op jit(solution)/shard_map/ppermute | solution.py:31
  13.8 0.9 fusion.2
  14.7 0.1 slice.33
  14.8 0.1 slice.34
  14.9 0.1 slice.35
  14.9 0.1 slice.36
  15.0 0.1 slice.37
  15.1 0.1 slice.38
  15.2 0.1 slice.39
  15.3 0.1 copy.34
  15.4 0.1 reshape.65
  15.5 0.1 copy.35
  15.5 0.1 reshape.66
  15.6 0.1 copy.36
  15.7 0.1 reshape.67
  15.8 0.1 copy.37
  15.9 0.1 reshape.68
  16.0 0.1 copy.38
  16.1 0.1 reshape.69
  16.2 0.1 copy.39
  16.3 0.1 reshape.70
  16.4 0.1 copy.40
  16.4 0.1 reshape.71
  16.6 0.1 copy.41
  16.8 1.6 %broadcast_in_dim.22 = bf16[32,2,9216]{2,1,0:T(2,128)(2,1)} broadcast(bf16[2,9216]{1,0:T(2,128)(2,1)S(1)} %constant_dynamic-update-slice_fusion), dimensions={1,2} | broadcast | bytes 1216512 | tf_op jit(solution)/shard_map/broadcast_in_dim | solution.py:267
  18.4 2.8 %all-to-all-start = ((bf16[32,2,9216]{2,1,0:T(2,128)(2,1)}), bf16[32,2,9216]{2,1,0:T(2,128)(2,1)S(1)}, u32[]{:S(2)}, u32[]{:S(2)}) async-start(bf16[32,2,9216]{2,1,0:T(2,128)(2,1)} %broadcast_in_dim.22), calls=%async_computation | async-start | bytes 2359296 | tf_op jit(solution)/shard_map/all_to_all | solution.py:268
  21.2 29.2 %shard_map.37.t_hbm = bf16[16,9216,128]{2,1,0:T(8,128)(2,1)} custom-call(s32[1]{0:T(128)} %bitcast.1.start_ref, bf16[128,128,512]{2,1,0:T(8,128)(2,1)} %l_hbm.3), custom_call_target="tpu_custom_call" | custom-call | flops 19327352832 | bytes 54525952 | tf_op jit(solution)/shard_map/pallas_call | solution.py:137
  50.5 0.1 all-to-all-done
  50.6 1.3 %all_to_all.9.s_ref = bf16[64,9216]{1,0:T(8,128)(2,1)} reshape(bf16[32,2,9216]{2,1,0:T(2,128)(2,1)S(1)} %all-to-all-done) | data formatting | bytes 2359296 | tf_op jit(solution)/shard_map/all_to_all | solution.py:268
  51.9 41.6 %shard_map.38 = bf16[64,32,128]{2,1,0:T(8,128)(2,1)} custom-call(s32[1]{0:T(128)} %bitcast.1.start_ref, bf16[128,128,512]{2,1,0:T(8,128)(2,1)} %l_hbm.3, bf16[16,9216,128]{2,1,0:T(8,128)(2,1)} %shard_map.37.t_hbm, bf16[64,9216]{1,0:T(8,128)(2,1)} %all_to_all.9.s_ref), custom_call_target="tpu_custom_call" | custom-call | flops 24159191040 | bytes 54525952 | tf_op jit(solution)/shard_map/pallas_call | solution.py:223
  93.5 0.0 copy-start
  93.5 21.5 %all_to_all.13 = bf16[64,32,128]{2,1,0:T(8,128)(2,1)S(1)} all-to-all(bf16[64,32,128]{2,1,0:T(8,128)(2,1)} %shard_map.38), channel_id=1, replica_groups=mesh['pi'=4,'pj'=8] {'pi','pj'}, dimensions={0} | all-to-all | bytes 1048576 | tf_op jit(solution)/shard_map/all_to_all | solution.py:252
  115.0 0.1 convert_reduce_fusion
  115.1 0.0 copy-done
  115.2 0.1 copy.44
  115.3 0.1 copy.43
  115.4 3.6 %collective-permute-start.2 = (bf16[128,128]{0,1:T(8,128)(2,1)S(1)}, bf16[128,128]{0,1:T(8,128)(2,1)S(1)}, u32[]{:S(2)}, u32[]{:S(2)}) collective-permute-start(bf16[128,128]{0,1:T(8,128)(2,1)S(1)} %bitcast.52), channel_id=1, source_target_pairs={{0,0},{1,1},{2,8},{3,9},{4,16},{5,17},{6,24},{7,25},{8,2},{9,3},{1... | collective-permute-start | bytes 98312 | tf_op jit(solution)/shard_map/ppermute | solution.py:31
  119.0 2.9 %collective-permute-start.3 = (bf16[128,128]{0,1:T(8,128)(2,1)S(1)}, bf16[128,128]{0,1:T(8,128)(2,1)S(1)}, u32[]{:S(2)}, u32[]{:S(2)}) collective-permute-start(bf16[128,128]{0,1:T(8,128)(2,1)S(1)} %bitcast.51), channel_id=1, source_target_pairs={{0,1},{1,0},{2,9},{3,8},{4,17},{5,16},{6,25},{7,24},{8,3},{9,2},{1... | collective-permute-start | bytes 98312 | tf_op jit(solution)/shard_map/ppermute | solution.py:31
  121.9 2.0 %collective-permute-done.2 = bf16[128,128]{0,1:T(8,128)(2,1)S(1)} collective-permute-done((bf16[128,128]{0,1:T(8,128)(2,1)S(1)}, bf16[128,128]{0,1:T(8,128)(2,1)S(1)}, u32[]{:S(2)}, u32[]{:S(2)}) %collective-permute-start.2) | collective-permute-done | bytes 32800 | tf_op jit(solution)/shard_map/ppermute | solution.py:31
  123.9 2.1 %collective-permute-done.3 = bf16[128,128]{0,1:T(8,128)(2,1)S(1)} collective-permute-done((bf16[128,128]{0,1:T(8,128)(2,1)S(1)}, bf16[128,128]{0,1:T(8,128)(2,1)S(1)}, u32[]{:S(2)}, u32[]{:S(2)}) %collective-permute-start.3) | collective-permute-done | bytes 32800 | tf_op jit(solution)/shard_map/ppermute | solution.py:31
  126.1 0.7 fusion.3
  (16 shorter events, 0.2 us)
Async XLA Ops:
  0.9 7.9 %collective-permute-start = (bf16[128,128]{0,1:T(8,128)(2,1)S(1)}, bf16[128,128]{0,1:T(8,128)(2,1)S(1)}, u32[]{:S(2)}, u32[]{:S(2)}) collective-permute-start(bf16[128,128]{0,1:T(8,128)(2,1)S(1)} %bitcast.49), channel_id=1, source_target_pairs={{0,0},{1,1},{2,8},{3,9},{4,16},{5,17},{6,24},{7,25},{8,2},{9,3},{1... | collective-permute-start | bytes 98312 | tf_op jit(solution)/shard_map/ppermute | solution.py:31
  6.8 7.0 %collective-permute-start.1 = (bf16[128,128]{0,1:T(8,128)(2,1)S(1)}, bf16[128,128]{0,1:T(8,128)(2,1)S(1)}, u32[]{:S(2)}, u32[]{:S(2)}) collective-permute-start(bf16[128,128]{0,1:T(8,128)(2,1)S(1)} %bitcast.50), channel_id=1, source_target_pairs={{0,1},{1,0},{2,9},{3,8},{4,17},{5,16},{6,25},{7,24},{8,3},{9,2},{1... | collective-permute-start | bytes 98312 | tf_op jit(solution)/shard_map/ppermute | solution.py:31
  18.4 32.2 %all-to-all-start = ((bf16[32,2,9216]{2,1,0:T(2,128)(2,1)}), bf16[32,2,9216]{2,1,0:T(2,128)(2,1)S(1)}, u32[]{:S(2)}, u32[]{:S(2)}) async-start(bf16[32,2,9216]{2,1,0:T(2,128)(2,1)} %broadcast_in_dim.22), calls=%async_computation | async-start | bytes 2359296 | tf_op jit(solution)/shard_map/all_to_all | solution.py:268
  93.5 21.6 %copy-start = (f32[2,1,128,128]{3,2,1,0:T(8,128)S(1)}, f32[2,1,128,128]{3,2,1,0:T(8,128)}, u32[]{:S(2)}) copy-start(f32[2,1,128,128]{3,2,1,0:T(8,128)} %param.5) | copy-start | bytes 393220
  115.4 8.5 %collective-permute-start.2 = (bf16[128,128]{0,1:T(8,128)(2,1)S(1)}, bf16[128,128]{0,1:T(8,128)(2,1)S(1)}, u32[]{:S(2)}, u32[]{:S(2)}) collective-permute-start(bf16[128,128]{0,1:T(8,128)(2,1)S(1)} %bitcast.52), channel_id=1, source_target_pairs={{0,0},{1,1},{2,8},{3,9},{4,16},{5,17},{6,24},{7,25},{8,2},{9,3},{1... | collective-permute-start | bytes 98312 | tf_op jit(solution)/shard_map/ppermute | solution.py:31
  119.0 7.0 %collective-permute-start.3 = (bf16[128,128]{0,1:T(8,128)(2,1)S(1)}, bf16[128,128]{0,1:T(8,128)(2,1)S(1)}, u32[]{:S(2)}, u32[]{:S(2)}) collective-permute-start(bf16[128,128]{0,1:T(8,128)(2,1)S(1)} %bitcast.51), channel_id=1, source_target_pairs={{0,1},{1,0},{2,9},{3,8},{4,17},{5,16},{6,25},{7,24},{8,3},{9,2},{1... | collective-permute-start | bytes 98312 | tf_op jit(solution)/shard_map/ppermute | solution.py:31

commit v4 on v2

v4 whole, which is shorter than its diff:
```python
import functools

import jax
import jax.numpy as jnp
from jax import lax
from jax.experimental import pallas as pl
from jax.experimental.pallas import tpu as pltpu
from jax.sharding import PartitionSpec as P


BOTH = ("pi", "pj")
GROUP = 16
NT = (((1,), (1,)), ((), ()))
NN = (((1,), (0,)), ((), ()))
ANY = pl.BlockSpec(memory_space=pl.ANY)
VMEM = pl.BlockSpec(memory_space=pltpu.VMEM)


def exchanged(block):
    pair_i = block.shape[0]
    count_i, count_j = lax.axis_size("pi"), lax.axis_size("pj")
    col = lax.axis_index("pj")
    arrived = []
    for shift in range(pair_i):
        route = []
        for row in range(count_i):
            for at in range(count_j):
                to = (at // pair_i) * count_j + pair_i * row + (at + shift) % pair_i
                route.append((row * count_j + at, to))
        sent = lax.dynamic_index_in_dim(block, (col + shift) % pair_i, 0, keepdims=False)
        arrived.append(lax.ppermute(sent, BOTH, route))
    return arrived


def mirrored(block):
    pair_i = block.shape[0]
    stacked = jnp.stack(exchanged(block))
    col = lax.axis_index("pj")
    return jnp.stack(
        [
            lax.dynamic_index_in_dim(stacked, (col - slot) % pair_i, 0, keepdims=False)
            for slot in range(pair_i)
        ]
    )


def groups(width):
    blocks = width // GROUP
    middle = (blocks - 2) // 2
    return [(k, blocks - 2 - k) for k in range(middle)] + [(middle,), (blocks - 1,)]


def group_rows(width):
    at = [0]
    for group in groups(width):
        at.append(at[-1] + GROUP * GROUP * sum(k + 1 for k in group) // width)
    return at


def place(width, group, k, d):
    high = GROUP * (k + 1)
    if len(group) == 2:
        return d * width + (0 if k == group[0] else width - high)
    wrap = GROUP * high // width
    return d % wrap * width + d // wrap * high


def pack_kernel(col_ref, own_ref, *refs):
    pair_i, width, _ = own_ref.shape
    arrived, out_ref, packed = refs[:pair_i], refs[pair_i], refs[pair_i + 1]
    d = lax.broadcasted_iota(jnp.int32, (width, width), 0)
    c = lax.broadcasted_iota(jnp.int32, (width, width), 1)
    weight = jnp.where(c < d, 1.0, jnp.where(c == d, 0.5, 0.0)).astype(jnp.float32)
    rows = group_rows(width)
    for slot in range(pair_i):
        which = lax.rem(col_ref[0] - slot + pair_i, pair_i)
        back = arrived[0][...].astype(jnp.float32)
        for m in range(1, pair_i):
            back = jnp.where(which == m, arrived[m][...].astype(jnp.float32), back)
        total = (jnp.swapaxes(own_ref[slot].astype(jnp.float32), 0, 1) + back) * weight
        for g, group in enumerate(groups(width)):
            lines = rows[g + 1] - rows[g]
            value = 0.0
            for k in group:
                for first in range(0, GROUP, lines):
                    low = place(width, group, k, first)
                    part = total[GROUP * k + first : GROUP * k + first + lines]
                    value = value + (pltpu.roll(part, low, 1) if low else part)
            packed[slot, rows[g] : rows[g + 1]] = value
    final = packed[...].astype(jnp.bfloat16)

    def copy(at, carry):
        out_ref[at] = final
        return carry

    lax.fori_loop(0, out_ref.shape[0], copy, 0)


def packed_copies(pairs, devices):
    pair_i, width, _ = pairs.shape
    lines = group_rows(width)[-1]
    arrived = exchanged(pairs)
    return pl.pallas_call(
        pack_kernel,
        out_shape=jax.ShapeDtypeStruct((devices, pair_i, lines, width), jnp.bfloat16),
        in_specs=[pl.BlockSpec(memory_space=pltpu.SMEM)] + [VMEM] * (1 + pair_i),
        out_specs=VMEM,
        scratch_shapes=[pltpu.VMEM((pair_i, lines, width), jnp.float32)],
        compiler_params=pltpu.CompilerParams(vmem_limit_bytes=40 << 20),
    )(lax.axis_index("pj").reshape(1), pairs, *arrived)


AHEAD = 3


def loads(start, rows, l_hbm, own, vectors, sems):
    width = vectors.shape[0]
    first = pltpu.make_async_copy(l_hbm.at[pl.ds(start, rows)], own, sems.at[width // GROUP])
    copies = []
    for k in [k for group in groups(width) for k in group]:
        part = pl.ds(k * GROUP, GROUP)
        copies.append(pltpu.make_async_copy(l_hbm.at[part], vectors.at[part], sems.at[k]))
    first.start()
    for copy in copies[:AHEAD]:
        copy.start()
    first.wait()
    return copies


def arrive(copies, n):
    copies[n].wait()
    if n + AHEAD < len(copies):
        copies[n + AHEAD].start()


def form(own, vectors, tile, group, k):
    rows, width, depth = own.shape
    high = GROUP * (k + 1)
    chunk = min(16 if 2 * high <= width else 8, rows)

    def step(at, carry):
        if chunk == rows:
            left = own[:, :high, :]
            part = slice(None)
        else:
            part = pl.ds(pl.multiple_of(at * chunk, chunk), chunk)
            left = own[part, :high, :]
        left = left.reshape(chunk * high, depth)
        for d in range(0, GROUP, 2):
            right = vectors[pl.ds(k * GROUP + d, 2)].reshape(2 * width, depth)
            product = lax.dot_general(left, right, NT, preferred_element_type=jnp.float32)
            product = product.astype(jnp.bfloat16)
            for q in range(2):
                value = product[:, q * width : (q + 1) * width].reshape(chunk, high, width)
                tile[part, pl.ds(place(width, group, k, d + q), high)] = value
        return carry

    if chunk == rows:
        step(0, 0)
    else:
        lax.fori_loop(0, rows // chunk, step, 0)


def tile_kernel(start_ref, l_hbm, t_hbm, vectors, own, tile, sems, sent):
    rows, width, _ = own.shape
    lines = group_rows(width)
    copies = loads(start_ref[0], rows, l_hbm, own, vectors, sems)
    n = 0
    outs = []
    for g, group in enumerate(groups(width)):
        if g >= 2:
            outs[g - 2].wait()
        for k in group:
            arrive(copies, n)
            n += 1
            form(own, vectors, tile.at[g % 2], group, k)
        low, size = lines[g] * width, (lines[g + 1] - lines[g]) * width
        outs.append(
            pltpu.make_async_copy(
                tile.at[g % 2, :, pl.ds(0, size)], t_hbm.at[:, pl.ds(low, size)], sent.at[g % 2]
            )
        )
        outs[g].start()
    for copy in outs[-2:]:
        copy.wait()


def tiles(cholesky, start, rows):
    width, _, depth = cholesky.shape
    size = group_rows(width)[-1] * width
    return pl.pallas_call(
        tile_kernel,
        out_shape=jax.ShapeDtypeStruct((rows, size, width), jnp.bfloat16),
        grid_spec=pltpu.PrefetchScalarGridSpec(
            num_scalar_prefetch=1,
            grid=(),
            in_specs=[ANY],
            out_specs=ANY,
            scratch_shapes=[
                pltpu.VMEM((width, width, depth), jnp.bfloat16),
                pltpu.VMEM((rows, width, depth), jnp.bfloat16),
                pltpu.VMEM((2, rows, GROUP * width, width), jnp.bfloat16),
                pltpu.SemaphoreType.DMA((width // GROUP + 1,)),
                pltpu.SemaphoreType.DMA((2,)),
            ],
        ),
        compiler_params=pltpu.CompilerParams(vmem_limit_bytes=60 << 20),
        cost_estimate=pl.CostEstimate(
            flops=2 * rows * width * size * depth,
            bytes_accessed=2 * width * width * depth + 2 * rows * size * width,
            transcendentals=0,
        ),
    )(start, cholesky)


def ladder_kernel(
    early, start_ref, l_hbm, t_hbm, s_ref, out_ref, vectors, own, tile, ring, total, sems, got
):
    late, width, _ = own.shape
    slots = ring.shape[0]
    lines = group_rows(width)
    copies = loads(start_ref[0] + early, late, l_hbm, own, vectors, sems)

    def fetch(a):
        slot = lax.rem(a, slots)
        return pltpu.make_async_copy(t_hbm.at[a], ring.at[slot], got.at[slot])

    n = 0
    for g, group in enumerate(groups(width)):
        for k in group:
            arrive(copies, n)
            n += 1
            if n == len(copies):
                for a in range(slots):
                    fetch(a).start()
            form(own, vectors, tile, group, k)
        size = (lines[g + 1] - lines[g]) * width
        weights = s_ref[:, lines[g] * width : lines[g + 1] * width]
        batch = min(8, late)

        def apply(at, carry, g=g, size=size, weights=weights):
            for q in range(0, batch, 2):
                a = at * batch + q
                both = jnp.concatenate([tile[a, :size], tile[a + 1, :size]], axis=1)
                value = lax.dot_general(weights, both, NN, preferred_element_type=jnp.float32)
                for h in range(2):
                    part = value[:, h * width : (h + 1) * width]
                    if g == 0:
                        total[early + a + h] = part
                    else:
                        total[early + a + h] += part
            return carry

        lax.fori_loop(0, late // batch, apply, 0)

    def rest(at, carry):
        a = 2 * at
        fetch(a).wait()
        fetch(a + 1).wait()
        both = jnp.concatenate([ring[lax.rem(a, slots)], ring[lax.rem(a + 1, slots)]], axis=1)
        value = lax.dot_general(s_ref[...], both, NN, preferred_element_type=jnp.float32)
        total[a] = value[:, :width]
        total[a + 1] = value[:, width:]
        pl.when(a + slots < early)(lambda: fetch(a + slots).start())
        pl.when(a + 1 + slots < early)(lambda: fetch(a + 1 + slots).start())
        return carry

    lax.fori_loop(0, early // 2, rest, 0)
    out_ref[...] = jnp.swapaxes(total[...], 0, 1).astype(out_ref.dtype)


def ladder(cholesky, tile, weights, start, rows):
    width, _, depth = cholesky.shape
    early = tile.shape[0]
    late = rows - early
    pairs, size = weights.shape
    slots = min(early, 8)
    return pl.pallas_call(
        functools.partial(ladder_kernel, early),
        out_shape=jax.ShapeDtypeStruct((pairs, rows, width), jnp.bfloat16),
        grid_spec=pltpu.PrefetchScalarGridSpec(
            num_scalar_prefetch=1,
            grid=(),
            in_specs=[ANY, ANY, VMEM],
            out_specs=VMEM,
            scratch_shapes=[
                pltpu.VMEM((width, width, depth), jnp.bfloat16),
                pltpu.VMEM((late, width, depth), jnp.bfloat16),
                pltpu.VMEM((late, GROUP * width, width), jnp.bfloat16),
                pltpu.VMEM((slots, size, width), jnp.bfloat16),
                pltpu.VMEM((rows, pairs, width), jnp.float32),
                pltpu.SemaphoreType.DMA((width // GROUP + 1,)),
                pltpu.SemaphoreType.DMA((slots,)),
            ],
        ),
        compiler_params=pltpu.CompilerParams(vmem_limit_bytes=62 << 20),
        cost_estimate=pl.CostEstimate(
            flops=2 * width * size * (late * depth + rows * pairs),
            bytes_accessed=2 * width * width * depth + 2 * early * size * width,
            transcendentals=0,
        ),
    )(start, cholesky, tile, weights)


def collected(sums):
    count_i, count_j = lax.axis_size("pi"), lax.axis_size("pj")
    landed = lax.all_to_all(sums, BOTH, split_axis=0, concat_axis=0, tiled=True)
    landed = landed.reshape((count_i, count_j, -1) + landed.shape[1:]).astype(jnp.float32)
    return jnp.sum(landed, axis=1)


def shards(amplitudes, cholesky, other_terms):
    width = cholesky.shape[0]
    pair_i, pair_j = amplitudes.shape[:2]
    count_i, count_j = lax.axis_size("pi"), lax.axis_size("pj")
    devices = count_i * count_j
    assert pair_j == 1 and pair_i * count_i == count_j
    rows = width // count_i
    early = rows // 2
    start = (lax.axis_index("pi") * rows).reshape(1)
    copies = packed_copies(amplitudes.reshape(pair_i, width, width), devices)
    weights = lax.all_to_all(copies, BOTH, split_axis=0, concat_axis=0, tiled=True)
    weights = weights.reshape(devices * pair_i, -1)
    tile = tiles(cholesky, start, early)
    part = collected(ladder(cholesky, tile, weights, start, rows))
    part = jnp.swapaxes(part, 0, 1).reshape(pair_i, width, width)
    half = other_terms.reshape(pair_i, width, width) + 0.5 * part
    back = mirrored(half.astype(jnp.bfloat16))
    total = half + jnp.swapaxes(back, 1, 2).astype(jnp.float32)
    return total.reshape(other_terms.shape)


def solution(mesh):
    return jax.shard_map(
        shards,
        mesh=mesh,
        in_specs=(P("pi", "pj", None, None), P(None, None, "pj"), P("pi", "pj", None, None)),
        out_specs=P("pi", "pj", None, None),
        check_vma=False,
    )
```

time: 135 us -> 124 us (0.919)
  blocking collectives: 27.4 us -> 20.3 us
  local copies, waits for them, and re-layouts: 6.19 us -> 3.1 us
    all_to_all x1, blocking collectives: 27.4 us -> 20.3 us  [collected(): landed = lax.all_to_all(sums, BOTH, split_axis=0, concat_axis=0, tiled=True)]
    unnamed x9 -> x5, local copies, waits for them, and re-layouts: 0.09 us -> 2.07 us
    broadcast_in_dim x1 -> x0, local copies, waits for them, and re-layouts: 1.64 us -> none  [shards(): jnp.broadcast_to(own[None], (devices,) + own.shape)]
    pallas_call x2 -> x3, Pallas kernels: 72.8 us -> 73.8 us  [the longest x1 43 us: ladder(): pl.pallas_call(functools.partial(ladder_kernel, early), out_shape=jax.Sha...]
  transfers between devices with their start and end apart: 5 -> 5, of which waited for: 5 -> 3; matrix products, arithmetic and copies ran while one was open for 0% -> 0% of each run, Pallas kernels for 22% -> 24%
where the time goes in v4:
time: 124 us
  Pallas kernels  73.8 us (60%)
  blocking collectives  20.3 us (16%)
  starting transfers between devices  16.2 us (13%)
  waiting for transfers between devices  9.54 us (8%)
  local copies, waits for them, and re-layouts  3.1 us (2%)
    pallas_call x1, Pallas kernels, ladder(): pl.pallas_call(functools.partial(ladder_kernel, early), out_shape=jax.Sha...  43 us
    pallas_call x1, Pallas kernels, tiles(): pl.pallas_call(tile_kernel, out_shape=jax.ShapeDtypeStruct((rows, size, w...  29.3 us
    all_to_all x1, blocking collectives, collected(): landed = lax.all_to_all(sums, BOTH, split_axis=0, concat_axis=0, tiled=True)  20.3 us
    ppermute x4, starting transfers between devices, exchanged(): arrived.append(lax.ppermute(sent, BOTH, route))  13.8 us
    ppermute x4, waiting for transfers between devices, exchanged(): arrived.append(lax.ppermute(sent, BOTH, route))  9.54 us
  transfers between devices with their start and end apart: 5, of which 3 were waited for; matrix products, arithmetic and copies ran while one was open for 0% of the time, Pallas kernels for 24%

profile of v4, /device:TPU:3, one launch (start us, length us, event | category | flops | bytes accessed | tf_op | source)
XLA Modules:
  0.0 123.9 jit_solution(4792332520513032384)
XLA Ops:
  0.0 0.8 dynamic-slice_bitcast_fusion
  0.8 4.8 %collective-permute-start.1 = (bf16[128,128]{1,0:T(8,128)(2,1)S(1)}, bf16[128,128]{1,0:T(8,128)(2,1)S(1)}, u32[]{:S(2)}, u32[]{:S(2)}) collective-permute-start(bf16[128,128]{1,0:T(8,128)(2,1)S(1)} %get-tuple-element.9), channel_id=1, source_target_pairs={{0,1},{1,0},{2,9},{3,8},{4,17},{5,16},{6,25},{7,24},{8,3},{9,2},{1... | collective-permute-start | bytes 98312 | tf_op jit(solution)/shard_map/ppermute | solution.py:31
  5.6 2.5 %collective-permute-start = (bf16[128,128]{1,0:T(8,128)(2,1)S(1)}, bf16[128,128]{1,0:T(8,128)(2,1)S(1)}, u32[]{:S(2)}, u32[]{:S(2)}) collective-permute-start(bf16[128,128]{1,0:T(8,128)(2,1)S(1)} %get-tuple-element.10), channel_id=1, source_target_pairs={{0,0},{1,1},{2,8},{3,9},{4,16},{5,17},{6,24},{7,25},{8,2},{9,3},{1... | collective-permute-start | bytes 98312 | tf_op jit(solution)/shard_map/ppermute | solution.py:31
  8.1 0.0 collective-permute-done.1.refs_1_
  8.1 5.4 %collective-permute-done.refs_0_ = bf16[128,128]{1,0:T(8,128)(2,1)S(1)} collective-permute-done((bf16[128,128]{1,0:T(8,128)(2,1)S(1)}, bf16[128,128]{1,0:T(8,128)(2,1)S(1)}, u32[]{:S(2)}, u32[]{:S(2)}) %collective-permute-start) | collective-permute-done | bytes 32800 | tf_op jit(solution)/shard_map/ppermute | solution.py:31
  13.5 0.0 copy-start
  13.5 0.8 copy-done
  14.3 1.4 %shard_map.38 = bf16[32,2,72,128]{3,2,1,0:T(8,128)(2,1)} custom-call(s32[1]{0:T(128)} %bitcast.2.col_ref, bf16[2,128,128]{2,1,0:T(8,128)(2,1)S(1)} %bitcast.40, bf16[128,128]{1,0:T(8,128)(2,1)S(1)} %collective-permute-done.refs_0_, bf16[128,128]{1,0:T(8,128)(2,1)S(1)} %collective-permute-done.1.refs_1_), custom_call_target="tpu_custom_call" | custom-call | tf_op jit(solution)/shard_map/pallas_call | solution.py:103
  15.7 2.4 %all-to-all-start = ((bf16[32,2,72,128]{3,2,1,0:T(8,128)(2,1)}), bf16[32,2,72,128]{3,2,1,0:T(8,128)(2,1)S(1)}, u32[]{:S(2)}, u32[]{:S(2)}) async-start(bf16[32,2,72,128]{3,2,1,0:T(8,128)(2,1)} %shard_map.38), calls=%async_computation | async-start | bytes 2359296 | tf_op jit(solution)/shard_map/all_to_all | solution.py:322
  18.1 29.3 %shard_map.37.t_hbm = bf16[16,9216,128]{2,1,0:T(8,128)(2,1)} custom-call(s32[1]{0:T(128)} %bitcast.1.start_ref, bf16[128,128,512]{2,1,0:T(8,128)(2,1)} %l_hbm.3), custom_call_target="tpu_custom_call" | custom-call | flops 19327352832 | bytes 54525952 | tf_op jit(solution)/shard_map/pallas_call | solution.py:191
  47.5 0.0 all-to-all-done
  47.5 1.2 copy.14
  48.7 43.0 %shard_map.39 = bf16[64,32,128]{2,1,0:T(8,128)(2,1)} custom-call(s32[1]{0:T(128)} %bitcast.1.start_ref, bf16[128,128,512]{2,1,0:T(8,128)(2,1)} %l_hbm.3, bf16[16,9216,128]{2,1,0:T(8,128)(2,1)} %shard_map.37.t_hbm, bf16[64,9216]{1,0:T(8,128)(2,1)} %bitcast.43), custom_call_target="tpu_custom_call" | custom-call | flops 24159191040 | bytes 54525952 | tf_op jit(solution)/shard_map/pallas_call | solution.py:278
  91.8 0.0 copy-start.1
  91.8 20.3 %all_to_all.10 = bf16[64,32,128]{2,1,0:T(8,128)(2,1)S(1)} all-to-all(bf16[64,32,128]{2,1,0:T(8,128)(2,1)} %shard_map.39), channel_id=1, replica_groups=mesh['pi'=4,'pj'=8] {'pi','pj'}, dimensions={0} | all-to-all | bytes 1048576 | tf_op jit(solution)/shard_map/all_to_all | solution.py:307
  112.1 0.1 convert_reduce_fusion
  112.2 0.0 copy-done.1
  112.3 0.1 copy.10
  112.4 0.1 copy.9
  112.5 3.6 %collective-permute-start.2 = (bf16[128,128]{0,1:T(8,128)(2,1)S(1)}, bf16[128,128]{0,1:T(8,128)(2,1)S(1)}, u32[]{:S(2)}, u32[]{:S(2)}) collective-permute-start(bf16[128,128]{0,1:T(8,128)(2,1)S(1)} %bitcast.45), channel_id=1, source_target_pairs={{0,0},{1,1},{2,8},{3,9},{4,16},{5,17},{6,24},{7,25},{8,2},{9,3},{1... | collective-permute-start | bytes 98312 | tf_op jit(solution)/shard_map/ppermute | solution.py:31
  116.2 2.9 %collective-permute-start.3 = (bf16[128,128]{0,1:T(8,128)(2,1)S(1)}, bf16[128,128]{0,1:T(8,128)(2,1)S(1)}, u32[]{:S(2)}, u32[]{:S(2)}) collective-permute-start(bf16[128,128]{0,1:T(8,128)(2,1)S(1)} %bitcast.44), channel_id=1, source_target_pairs={{0,1},{1,0},{2,9},{3,8},{4,17},{5,16},{6,25},{7,24},{8,3},{9,2},{1... | collective-permute-start | bytes 98312 | tf_op jit(solution)/shard_map/ppermute | solution.py:31
  119.0 2.0 %collective-permute-done.2 = bf16[128,128]{0,1:T(8,128)(2,1)S(1)} collective-permute-done((bf16[128,128]{0,1:T(8,128)(2,1)S(1)}, bf16[128,128]{0,1:T(8,128)(2,1)S(1)}, u32[]{:S(2)}, u32[]{:S(2)}) %collective-permute-start.2) | collective-permute-done | bytes 32800 | tf_op jit(solution)/shard_map/ppermute | solution.py:31
  121.0 2.1 %collective-permute-done.3 = bf16[128,128]{0,1:T(8,128)(2,1)S(1)} collective-permute-done((bf16[128,128]{0,1:T(8,128)(2,1)S(1)}, bf16[128,128]{0,1:T(8,128)(2,1)S(1)}, u32[]{:S(2)}, u32[]{:S(2)}) %collective-permute-start.3) | collective-permute-done | bytes 32800 | tf_op jit(solution)/shard_map/ppermute | solution.py:31
  123.2 0.7 fusion
  (5 shorter events, 0.1 us)
Async XLA Ops:
  0.8 7.3 %collective-permute-start.1 = (bf16[128,128]{1,0:T(8,128)(2,1)S(1)}, bf16[128,128]{1,0:T(8,128)(2,1)S(1)}, u32[]{:S(2)}, u32[]{:S(2)}) collective-permute-start(bf16[128,128]{1,0:T(8,128)(2,1)S(1)} %get-tuple-element.9), channel_id=1, source_target_pairs={{0,1},{1,0},{2,9},{3,8},{4,17},{5,16},{6,25},{7,24},{8,3},{9,2},{1... | collective-permute-start | bytes 98312 | tf_op jit(solution)/shard_map/ppermute | solution.py:31
  5.6 7.9 %collective-permute-start = (bf16[128,128]{1,0:T(8,128)(2,1)S(1)}, bf16[128,128]{1,0:T(8,128)(2,1)S(1)}, u32[]{:S(2)}, u32[]{:S(2)}) collective-permute-start(bf16[128,128]{1,0:T(8,128)(2,1)S(1)} %get-tuple-element.10), channel_id=1, source_target_pairs={{0,0},{1,1},{2,8},{3,9},{4,16},{5,17},{6,24},{7,25},{8,2},{9,3},{1... | collective-permute-start | bytes 98312 | tf_op jit(solution)/shard_map/ppermute | solution.py:31
  13.5 0.8 copy-start
  15.7 31.8 %all-to-all-start = ((bf16[32,2,72,128]{3,2,1,0:T(8,128)(2,1)}), bf16[32,2,72,128]{3,2,1,0:T(8,128)(2,1)S(1)}, u32[]{:S(2)}, u32[]{:S(2)}) async-start(bf16[32,2,72,128]{3,2,1,0:T(8,128)(2,1)} %shard_map.38), calls=%async_computation | async-start | bytes 2359296 | tf_op jit(solution)/shard_map/all_to_all | solution.py:322
  91.8 20.5 %copy-start.1 = (f32[2,1,128,128]{3,2,1,0:T(8,128)S(1)}, f32[2,1,128,128]{3,2,1,0:T(8,128)}, u32[]{:S(2)}) copy-start(f32[2,1,128,128]{3,2,1,0:T(8,128)} %param.5) | copy-start | bytes 393220
  112.5 8.5 %collective-permute-start.2 = (bf16[128,128]{0,1:T(8,128)(2,1)S(1)}, bf16[128,128]{0,1:T(8,128)(2,1)S(1)}, u32[]{:S(2)}, u32[]{:S(2)}) collective-permute-start(bf16[128,128]{0,1:T(8,128)(2,1)S(1)} %bitcast.45), channel_id=1, source_target_pairs={{0,0},{1,1},{2,8},{3,9},{4,16},{5,17},{6,24},{7,25},{8,2},{9,3},{1... | collective-permute-start | bytes 98312 | tf_op jit(solution)/shard_map/ppermute | solution.py:31
  116.2 7.0 %collective-permute-start.3 = (bf16[128,128]{0,1:T(8,128)(2,1)S(1)}, bf16[128,128]{0,1:T(8,128)(2,1)S(1)}, u32[]{:S(2)}, u32[]{:S(2)}) collective-permute-start(bf16[128,128]{0,1:T(8,128)(2,1)S(1)} %bitcast.44), channel_id=1, source_target_pairs={{0,1},{1,0},{2,9},{3,8},{4,17},{5,16},{6,25},{7,24},{8,3},{9,2},{1... | collective-permute-start | bytes 98312 | tf_op jit(solution)/shard_map/ppermute | solution.py:31

commit v5 on v4

--- a/solution.py
+++ b/solution.py
@@ -133,10 +133,10 @@
         copies[n + AHEAD].start()
 
 
-def form(own, vectors, tile, group, k):
+def form(own, vectors, tile, group, k, most):
     rows, width, depth = own.shape
     high = GROUP * (k + 1)
-    chunk = min(16 if 2 * high <= width else 8, rows)
+    chunk = min(16 if 2 * high <= width else most, rows)
 
     def step(at, carry):
         if chunk == rows:
@@ -173,7 +173,7 @@
         for k in group:
             arrive(copies, n)
             n += 1
-            form(own, vectors, tile.at[g % 2], group, k)
+            form(own, vectors, tile.at[g % 2], group, k, 8)
         low, size = lines[g] * width, (lines[g + 1] - lines[g]) * width
         outs.append(
             pltpu.make_async_copy(
@@ -233,22 +233,21 @@
             if n == len(copies):
                 for a in range(slots):
                     fetch(a).start()
-            form(own, vectors, tile, group, k)
+            form(own, vectors, tile, group, k, 16)
         size = (lines[g + 1] - lines[g]) * width
         weights = s_ref[:, lines[g] * width : lines[g + 1] * width]
-        batch = min(8, late)
+        batch = min(16, late)
 
         def apply(at, carry, g=g, size=size, weights=weights):
-            for q in range(0, batch, 2):
+            for q in range(batch):
                 a = at * batch + q
-                both = jnp.concatenate([tile[a, :size], tile[a + 1, :size]], axis=1)
-                value = lax.dot_general(weights, both, NN, preferred_element_type=jnp.float32)
-                for h in range(2):
-                    part = value[:, h * width : (h + 1) * width]
-                    if g == 0:
-                        total[early + a + h] = part
-                    else:
-                        total[early + a + h] += part
+                value = lax.dot_general(
+                    weights, tile[a, :size], NN, preferred_element_type=jnp.float32
+                )
+                if g == 0:
+                    total[early + a] = value
+                else:
+                    total[early + a] += value
             return carry
 
         lax.fori_loop(0, late // batch, apply, 0)

time: 124 us -> 121 us (0.976)
  Pallas kernels: 73.8 us -> 70.3 us
    pallas_call x1, Pallas kernels: 43 us -> 39.4 us  [ladder(): pl.pallas_call(functools.partial(ladder_kernel, early), out_shape=jax.Sha...]
  transfers between devices with their start and end apart: 5 -> 5, of which waited for: 3 -> 3; matrix products, arithmetic and copies ran while one was open for 0% -> 0% of each run, Pallas kernels for 24% -> 25%
where the time goes in v5:
time: 121 us; the launch traced here: 120 us
  Pallas kernels  70.3 us (58%)
  blocking collectives  20.3 us (17%)
  starting transfers between devices  16.2 us (13%)
  waiting for transfers between devices  9.54 us (8%)
  local copies, waits for them, and re-layouts  3.1 us (3%)
    pallas_call x1, Pallas kernels, ladder(): pl.pallas_call(functools.partial(ladder_kernel, early), out_shape=jax.Sha...  39.4 us
    pallas_call x1, Pallas kernels, tiles(): pl.pallas_call(tile_kernel, out_shape=jax.ShapeDtypeStruct((rows, size, w...  29.5 us
    all_to_all x1, blocking collectives, collected(): landed = lax.all_to_all(sums, BOTH, split_axis=0, concat_axis=0, tiled=True)  20.3 us
    ppermute x4, starting transfers between devices, exchanged(): arrived.append(lax.ppermute(sent, BOTH, route))  13.8 us
    ppermute x4, waiting for transfers between devices, exchanged(): arrived.append(lax.ppermute(sent, BOTH, route))  9.54 us
  transfers between devices with their start and end apart: 5, of which 3 were waited for; matrix products, arithmetic and copies ran while one was open for 0% of the time, Pallas kernels for 25%

profile of v5, /device:TPU:3, one launch (start us, length us, event | category | flops | bytes accessed | tf_op | source)
XLA Modules:
  0.0 120.4 jit_solution(843499802669513106)
XLA Ops:
  0.0 0.8 dynamic-slice_bitcast_fusion
  0.8 4.8 %collective-permute-start.1 = (bf16[128,128]{1,0:T(8,128)(2,1)S(1)}, bf16[128,128]{1,0:T(8,128)(2,1)S(1)}, u32[]{:S(2)}, u32[]{:S(2)}) collective-permute-start(bf16[128,128]{1,0:T(8,128)(2,1)S(1)} %get-tuple-element.9), channel_id=1, source_target_pairs={{0,1},{1,0},{2,9},{3,8},{4,17},{5,16},{6,25},{7,24},{8,3},{9,2},{1... | collective-permute-start | bytes 98312 | tf_op jit(solution)/shard_map/ppermute | solution.py:31
  5.6 2.5 %collective-permute-start = (bf16[128,128]{1,0:T(8,128)(2,1)S(1)}, bf16[128,128]{1,0:T(8,128)(2,1)S(1)}, u32[]{:S(2)}, u32[]{:S(2)}) collective-permute-start(bf16[128,128]{1,0:T(8,128)(2,1)S(1)} %get-tuple-element.10), channel_id=1, source_target_pairs={{0,0},{1,1},{2,8},{3,9},{4,16},{5,17},{6,24},{7,25},{8,2},{9,3},{1... | collective-permute-start | bytes 98312 | tf_op jit(solution)/shard_map/ppermute | solution.py:31
  8.1 0.0 collective-permute-done.1.refs_1_
  8.1 5.4 %collective-permute-done.refs_0_ = bf16[128,128]{1,0:T(8,128)(2,1)S(1)} collective-permute-done((bf16[128,128]{1,0:T(8,128)(2,1)S(1)}, bf16[128,128]{1,0:T(8,128)(2,1)S(1)}, u32[]{:S(2)}, u32[]{:S(2)}) %collective-permute-start) | collective-permute-done | bytes 32800 | tf_op jit(solution)/shard_map/ppermute | solution.py:31
  13.5 0.0 copy-start
  13.5 0.8 copy-done
  14.3 1.4 %shard_map.38 = bf16[32,2,72,128]{3,2,1,0:T(8,128)(2,1)} custom-call(s32[1]{0:T(128)} %bitcast.2.col_ref, bf16[2,128,128]{2,1,0:T(8,128)(2,1)S(1)} %bitcast.40, bf16[128,128]{1,0:T(8,128)(2,1)S(1)} %collective-permute-done.refs_0_, bf16[128,128]{1,0:T(8,128)(2,1)S(1)} %collective-permute-done.1.refs_1_), custom_call_target="tpu_custom_call" | custom-call | tf_op jit(solution)/shard_map/pallas_call | solution.py:103
  15.7 2.4 %all-to-all-start = ((bf16[32,2,72,128]{3,2,1,0:T(8,128)(2,1)}), bf16[32,2,72,128]{3,2,1,0:T(8,128)(2,1)S(1)}, u32[]{:S(2)}, u32[]{:S(2)}) async-start(bf16[32,2,72,128]{3,2,1,0:T(8,128)(2,1)} %shard_map.38), calls=%async_computation | async-start | bytes 2359296 | tf_op jit(solution)/shard_map/all_to_all | solution.py:321
  18.1 29.5 %shard_map.37.t_hbm = bf16[16,9216,128]{2,1,0:T(8,128)(2,1)} custom-call(s32[1]{0:T(128)} %bitcast.1.start_ref, bf16[128,128,512]{2,1,0:T(8,128)(2,1)} %l_hbm.3), custom_call_target="tpu_custom_call" | custom-call | flops 19327352832 | bytes 54525952 | tf_op jit(solution)/shard_map/pallas_call | solution.py:191
  47.7 0.0 all-to-all-done
  47.7 1.2 %copy.14 = bf16[8,8,72,128]{3,1,2,0:T(8,128)(2,1)} copy(bf16[8,8,72,128]{3,2,1,0:T(8,128)(2,1)S(1)} %bitcast.41) | data formatting | bytes 2359296
  48.9 39.4 %shard_map.39 = bf16[64,32,128]{2,1,0:T(8,128)(2,1)} custom-call(s32[1]{0:T(128)} %bitcast.1.start_ref, bf16[128,128,512]{2,1,0:T(8,128)(2,1)} %l_hbm.3, bf16[16,9216,128]{2,1,0:T(8,128)(2,1)} %shard_map.37.t_hbm, bf16[64,9216]{1,0:T(8,128)(2,1)} %bitcast.43), custom_call_target="tpu_custom_call" | custom-call | flops 24159191040 | bytes 54525952 | tf_op jit(solution)/shard_map/pallas_call | solution.py:277
  88.3 0.0 copy-start.1
  88.3 20.3 %all_to_all.10 = bf16[64,32,128]{2,1,0:T(8,128)(2,1)S(1)} all-to-all(bf16[64,32,128]{2,1,0:T(8,128)(2,1)} %shard_map.39), channel_id=1, replica_groups=mesh['pi'=4,'pj'=8] {'pi','pj'}, dimensions={0} | all-to-all | bytes 1048576 | tf_op jit(solution)/shard_map/all_to_all | solution.py:306
  108.7 0.1 convert_reduce_fusion
  108.8 0.0 copy-done.1
  108.8 0.1 copy.10
  108.9 0.1 copy.9
  109.1 3.6 %collective-permute-start.2 = (bf16[128,128]{0,1:T(8,128)(2,1)S(1)}, bf16[128,128]{0,1:T(8,128)(2,1)S(1)}, u32[]{:S(2)}, u32[]{:S(2)}) collective-permute-start(bf16[128,128]{0,1:T(8,128)(2,1)S(1)} %bitcast.45), channel_id=1, source_target_pairs={{0,0},{1,1},{2,8},{3,9},{4,16},{5,17},{6,24},{7,25},{8,2},{9,3},{1... | collective-permute-start | bytes 98312 | tf_op jit(solution)/shard_map/ppermute | solution.py:31
  112.7 2.9 %collective-permute-start.3 = (bf16[128,128]{0,1:T(8,128)(2,1)S(1)}, bf16[128,128]{0,1:T(8,128)(2,1)S(1)}, u32[]{:S(2)}, u32[]{:S(2)}) collective-permute-start(bf16[128,128]{0,1:T(8,128)(2,1)S(1)} %bitcast.44), channel_id=1, source_target_pairs={{0,1},{1,0},{2,9},{3,8},{4,17},{5,16},{6,25},{7,24},{8,3},{9,2},{1... | collective-permute-start | bytes 98312 | tf_op jit(solution)/shard_map/ppermute | solution.py:31
  115.6 2.0 %collective-permute-done.2 = bf16[128,128]{0,1:T(8,128)(2,1)S(1)} collective-permute-done((bf16[128,128]{0,1:T(8,128)(2,1)S(1)}, bf16[128,128]{0,1:T(8,128)(2,1)S(1)}, u32[]{:S(2)}, u32[]{:S(2)}) %collective-permute-start.2) | collective-permute-done | bytes 32800 | tf_op jit(solution)/shard_map/ppermute | solution.py:31
  117.6 2.1 %collective-permute-done.3 = bf16[128,128]{0,1:T(8,128)(2,1)S(1)} collective-permute-done((bf16[128,128]{0,1:T(8,128)(2,1)S(1)}, bf16[128,128]{0,1:T(8,128)(2,1)S(1)}, u32[]{:S(2)}, u32[]{:S(2)}) %collective-permute-start.3) | collective-permute-done | bytes 32800 | tf_op jit(solution)/shard_map/ppermute | solution.py:31
  119.7 0.7 fusion
  (5 shorter events, 0.1 us)
Async XLA Ops:
  0.8 7.3 %collective-permute-start.1 = (bf16[128,128]{1,0:T(8,128)(2,1)S(1)}, bf16[128,128]{1,0:T(8,128)(2,1)S(1)}, u32[]{:S(2)}, u32[]{:S(2)}) collective-permute-start(bf16[128,128]{1,0:T(8,128)(2,1)S(1)} %get-tuple-element.9), channel_id=1, source_target_pairs={{0,1},{1,0},{2,9},{3,8},{4,17},{5,16},{6,25},{7,24},{8,3},{9,2},{1... | collective-permute-start | bytes 98312 | tf_op jit(solution)/shard_map/ppermute | solution.py:31
  5.6 7.9 %collective-permute-start = (bf16[128,128]{1,0:T(8,128)(2,1)S(1)}, bf16[128,128]{1,0:T(8,128)(2,1)S(1)}, u32[]{:S(2)}, u32[]{:S(2)}) collective-permute-start(bf16[128,128]{1,0:T(8,128)(2,1)S(1)} %get-tuple-element.10), channel_id=1, source_target_pairs={{0,0},{1,1},{2,8},{3,9},{4,16},{5,17},{6,24},{7,25},{8,2},{9,3},{1... | collective-permute-start | bytes 98312 | tf_op jit(solution)/shard_map/ppermute | solution.py:31
  13.5 0.8 copy-start
  15.7 31.9 %all-to-all-start = ((bf16[32,2,72,128]{3,2,1,0:T(8,128)(2,1)}), bf16[32,2,72,128]{3,2,1,0:T(8,128)(2,1)S(1)}, u32[]{:S(2)}, u32[]{:S(2)}) async-start(bf16[32,2,72,128]{3,2,1,0:T(8,128)(2,1)} %shard_map.38), calls=%async_computation | async-start | bytes 2359296 | tf_op jit(solution)/shard_map/all_to_all | solution.py:321
  88.3 20.5 %copy-start.1 = (f32[2,1,128,128]{3,2,1,0:T(8,128)S(1)}, f32[2,1,128,128]{3,2,1,0:T(8,128)}, u32[]{:S(2)}) copy-start(f32[2,1,128,128]{3,2,1,0:T(8,128)} %param.5) | copy-start | bytes 393220
  109.1 8.5 %collective-permute-start.2 = (bf16[128,128]{0,1:T(8,128)(2,1)S(1)}, bf16[128,128]{0,1:T(8,128)(2,1)S(1)}, u32[]{:S(2)}, u32[]{:S(2)}) collective-permute-start(bf16[128,128]{0,1:T(8,128)(2,1)S(1)} %bitcast.45), channel_id=1, source_target_pairs={{0,0},{1,1},{2,8},{3,9},{4,16},{5,17},{6,24},{7,25},{8,2},{9,3},{1... | collective-permute-start | bytes 98312 | tf_op jit(solution)/shard_map/ppermute | solution.py:31
  112.7 7.0 %collective-permute-start.3 = (bf16[128,128]{0,1:T(8,128)(2,1)S(1)}, bf16[128,128]{0,1:T(8,128)(2,1)S(1)}, u32[]{:S(2)}, u32[]{:S(2)}) collective-permute-start(bf16[128,128]{0,1:T(8,128)(2,1)S(1)} %bitcast.44), channel_id=1, source_target_pairs={{0,1},{1,0},{2,9},{3,8},{4,17},{5,16},{6,25},{7,24},{8,3},{9,2},{1... | collective-permute-start | bytes 98312 | tf_op jit(solution)/shard_map/ppermute | solution.py:31

commit v6 on v5

--- a/solution.py
+++ b/solution.py
@@ -20,7 +20,7 @@
     pair_i = block.shape[0]
     count_i, count_j = lax.axis_size("pi"), lax.axis_size("pj")
     col = lax.axis_index("pj")
-    arrived = []
+    own, arrived = [], []
     for shift in range(pair_i):
         route = []
         for row in range(count_i):
@@ -28,13 +28,14 @@
                 to = (at // pair_i) * count_j + pair_i * row + (at + shift) % pair_i
                 route.append((row * count_j + at, to))
         sent = lax.dynamic_index_in_dim(block, (col + shift) % pair_i, 0, keepdims=False)
+        own.append(sent)
         arrived.append(lax.ppermute(sent, BOTH, route))
-    return arrived
+    return own, arrived
 
 
 def mirrored(block):
     pair_i = block.shape[0]
-    stacked = jnp.stack(exchanged(block))
+    stacked = jnp.stack(exchanged(block)[1])
     col = lax.axis_index("pj")
     return jnp.stack(
         [
@@ -47,7 +48,7 @@
 def groups(width):
     blocks = width // GROUP
     middle = (blocks - 2) // 2
-    return [(k, blocks - 2 - k) for k in range(middle)] + [(middle,), (blocks - 1,)]
+    return [(blocks - 1,)] + [(k, blocks - 2 - k) for k in range(middle)] + [(middle,)]
 
 
 def group_rows(width):
@@ -65,19 +66,26 @@
     return d % wrap * width + d // wrap * high
 
 
-def pack_kernel(col_ref, own_ref, *refs):
-    pair_i, width, _ = own_ref.shape
-    arrived, out_ref, packed = refs[:pair_i], refs[pair_i], refs[pair_i + 1]
+def chosen(refs, which):
+    value = refs[0][...].astype(jnp.float32)
+    for m in range(1, len(refs)):
+        value = jnp.where(which == m, refs[m][...].astype(jnp.float32), value)
+    return value
+
+
+def pack_kernel(pair_i, col_ref, *refs):
+    own, arrived = refs[:pair_i], refs[pair_i : 2 * pair_i]
+    out_ref, packed = refs[2 * pair_i :]
+    width = own[0].shape[0]
+    turn = lax.rem(col_ref[0], pair_i)
     d = lax.broadcasted_iota(jnp.int32, (width, width), 0)
     c = lax.broadcasted_iota(jnp.int32, (width, width), 1)
     weight = jnp.where(c < d, 1.0, jnp.where(c == d, 0.5, 0.0)).astype(jnp.float32)
     rows = group_rows(width)
     for slot in range(pair_i):
-        which = lax.rem(col_ref[0] - slot + pair_i, pair_i)
-        back = arrived[0][...].astype(jnp.float32)
-        for m in range(1, pair_i):
-            back = jnp.where(which == m, arrived[m][...].astype(jnp.float32), back)
-        total = (jnp.swapaxes(own_ref[slot].astype(jnp.float32), 0, 1) + back) * weight
+        mine = chosen(own, lax.rem(slot - turn + pair_i, pair_i))
+        back = chosen(arrived, lax.rem(turn - slot + pair_i, pair_i))
+        total = (jnp.swapaxes(mine, 0, 1) + back) * weight
         for g, group in enumerate(groups(width)):
             lines = rows[g + 1] - rows[g]
             value = 0.0
@@ -99,29 +107,29 @@
 def packed_copies(pairs, devices):
     pair_i, width, _ = pairs.shape
     lines = group_rows(width)[-1]
-    arrived = exchanged(pairs)
+    own, arrived = exchanged(pairs)
     return pl.pallas_call(
-        pack_kernel,
+        functools.partial(pack_kernel, pair_i),
         out_shape=jax.ShapeDtypeStruct((devices, pair_i, lines, width), jnp.bfloat16),
-        in_specs=[pl.BlockSpec(memory_space=pltpu.SMEM)] + [VMEM] * (1 + pair_i),
+        in_specs=[pl.BlockSpec(memory_space=pltpu.SMEM)] + [VMEM] * (2 * pair_i),
         out_specs=VMEM,
         scratch_shapes=[pltpu.VMEM((pair_i, lines, width), jnp.float32)],
         compiler_params=pltpu.CompilerParams(vmem_limit_bytes=40 << 20),
-    )(lax.axis_index("pj").reshape(1), pairs, *arrived)
+    )(lax.axis_index("pj").reshape(1), *own, *arrived)
 
 
 AHEAD = 3
 
 
-def loads(start, rows, l_hbm, own, vectors, sems):
+def loads(start, rows, l_hbm, own, vectors, sems, order):
     width = vectors.shape[0]
     first = pltpu.make_async_copy(l_hbm.at[pl.ds(start, rows)], own, sems.at[width // GROUP])
     copies = []
-    for k in [k for group in groups(width) for k in group]:
+    for k in [k for group in order for k in group]:
         part = pl.ds(k * GROUP, GROUP)
         copies.append(pltpu.make_async_copy(l_hbm.at[part], vectors.at[part], sems.at[k]))
     first.start()
-    for copy in copies[:AHEAD]:
+    for copy in copies[:2]:
         copy.start()
     first.wait()
     return copies
@@ -129,8 +137,8 @@
 
 def arrive(copies, n):
     copies[n].wait()
-    if n + AHEAD < len(copies):
-        copies[n + AHEAD].start()
+    for copy in copies[2 : 1 + AHEAD] if n == 0 else copies[n + AHEAD : n + AHEAD + 1]:
+        copy.start()
 
 
 def form(own, vectors, tile, group, k, most):
@@ -164,7 +172,7 @@
 def tile_kernel(start_ref, l_hbm, t_hbm, vectors, own, tile, sems, sent):
     rows, width, _ = own.shape
     lines = group_rows(width)
-    copies = loads(start_ref[0], rows, l_hbm, own, vectors, sems)
+    copies = loads(start_ref[0], rows, l_hbm, own, vectors, sems, groups(width))
     n = 0
     outs = []
     for g, group in enumerate(groups(width)):
@@ -219,14 +227,17 @@
     late, width, _ = own.shape
     slots = ring.shape[0]
     lines = group_rows(width)
-    copies = loads(start_ref[0] + early, late, l_hbm, own, vectors, sems)
+    order = groups(width)
+    order = order[1:] + order[:1]
+    copies = loads(start_ref[0] + early, late, l_hbm, own, vectors, sems, order)
 
     def fetch(a):
         slot = lax.rem(a, slots)
         return pltpu.make_async_copy(t_hbm.at[a], ring.at[slot], got.at[slot])
 
     n = 0
-    for g, group in enumerate(groups(width)):
+    for group in order:
+        g = groups(width).index(group)
         for k in group:
             arrive(copies, n)
             n += 1
@@ -238,13 +249,13 @@
         weights = s_ref[:, lines[g] * width : lines[g + 1] * width]
         batch = min(16, late)
 
-        def apply(at, carry, g=g, size=size, weights=weights):
+        def apply(at, carry, group=group, size=size, weights=weights):
             for q in range(batch):
                 a = at * batch + q
                 value = lax.dot_general(
                     weights, tile[a, :size], NN, preferred_element_type=jnp.float32
                 )
-                if g == 0:
+                if group is order[0]:
                     total[early + a] = value
                 else:
                     total[early + a] += value

time: 121 us -> 118 us (0.975)
  Pallas kernels: 70.3 us -> 67.5 us
  waiting for transfers between devices: 9.54 us -> 11.4 us
  blocking collectives: 20.3 us -> 19 us
    pallas_call x1, Pallas kernels: 29.5 us -> 26.8 us  [tiles(): pl.pallas_call(tile_kernel, out_shape=jax.ShapeDtypeStruct((rows, size, w...]
    all_to_all x1, waiting for transfers between devices: 0.01 us -> 2 us  [shards(): lax.all_to_all(copies, BOTH, split_axis=0, concat_axis=0, tiled=True)]
    all_to_all x1, blocking collectives: 20.3 us -> 19 us  [collected(): landed = lax.all_to_all(sums, BOTH, split_axis=0, concat_axis=0, tiled=True)]
  transfers between devices with their start and end apart: 5 -> 5, of which waited for: 3 -> 4; matrix products, arithmetic and copies ran while one was open for 0% -> 0% of each run, Pallas kernels for 25% -> 23%
where the time goes in v6:
time: 118 us; the launch traced here: 117 us
  Pallas kernels  67.5 us (57%)
  blocking collectives  19 us (16%)
  starting transfers between devices  16.2 us (14%)
  waiting for transfers between devices  11.4 us (10%)
  local copies, waits for them, and re-layouts  2.27 us (2%)
    pallas_call x1, Pallas kernels, ladder(): pl.pallas_call(functools.partial(ladder_kernel, early), out_shape=jax.Sha...  39.3 us
    pallas_call x1, Pallas kernels, tiles(): pl.pallas_call(tile_kernel, out_shape=jax.ShapeDtypeStruct((rows, size, w...  26.8 us
    all_to_all x1, blocking collectives, collected(): landed = lax.all_to_all(sums, BOTH, split_axis=0, concat_axis=0, tiled=True)  19 us
    ppermute x4, starting transfers between devices, exchanged(): arrived.append(lax.ppermute(sent, BOTH, route))  13.8 us
    ppermute x4, waiting for transfers between devices, exchanged(): arrived.append(lax.ppermute(sent, BOTH, route))  9.45 us
    all_to_all x1, starting transfers between devices, shards(): lax.all_to_all(copies, BOTH, split_axis=0, concat_axis=0, tiled=True)  2.4 us
  transfers between devices with their start and end apart: 5, of which 4 were waited for; matrix products, arithmetic and copies ran while one was open for 0% of the time, Pallas kernels for 23%

profile of v6, /device:TPU:3, one launch (start us, length us, event | category | flops | bytes accessed | tf_op | source)
XLA Modules:
  0.0 117.4 jit_solution(15161198495307438750)
XLA Ops:
  0.0 0.8 dynamic-slice_bitcast_fusion
  0.8 4.8 %collective-permute-start.1 = (bf16[128,128]{1,0:T(8,128)(2,1)S(1)}, bf16[128,128]{1,0:T(8,128)(2,1)S(1)}, u32[]{:S(2)}, u32[]{:S(2)}) collective-permute-start(bf16[128,128]{1,0:T(8,128)(2,1)S(1)} %get-tuple-element.9.refs_1_), channel_id=1, source_target_pairs={{0,1},{1,0},{2,9},{3,8},{4,17},{5,16},{6,25},{7,24},{8,3},{9,2},{1... | collective-permute-start | bytes 98312 | tf_op jit(solution)/shard_map/ppermute | solution.py:32
  5.6 2.5 %collective-permute-start = (bf16[128,128]{1,0:T(8,128)(2,1)S(1)}, bf16[128,128]{1,0:T(8,128)(2,1)S(1)}, u32[]{:S(2)}, u32[]{:S(2)}) collective-permute-start(bf16[128,128]{1,0:T(8,128)(2,1)S(1)} %get-tuple-element.10.refs_0_), channel_id=1, source_target_pairs={{0,0},{1,1},{2,8},{3,9},{4,16},{5,17},{6,24},{7,25},{8,2},{9,3},{1... | collective-permute-start | bytes 98312 | tf_op jit(solution)/shard_map/ppermute | solution.py:32
  8.1 0.0 collective-permute-done.1.refs_3_
  8.1 5.4 %collective-permute-done.refs_2_ = bf16[128,128]{1,0:T(8,128)(2,1)S(1)} collective-permute-done((bf16[128,128]{1,0:T(8,128)(2,1)S(1)}, bf16[128,128]{1,0:T(8,128)(2,1)S(1)}, u32[]{:S(2)}, u32[]{:S(2)}) %collective-permute-start) | collective-permute-done | bytes 32800 | tf_op jit(solution)/shard_map/ppermute | solution.py:32
  13.5 1.4 %shard_map.38 = bf16[32,2,72,128]{3,2,1,0:T(8,128)(2,1)} custom-call(s32[1]{0:T(128)} %bitcast.2.col_ref, bf16[128,128]{1,0:T(8,128)(2,1)S(1)} %get-tuple-element.10.refs_0_, bf16[128,128]{1,0:T(8,128)(2,1)S(1)} %get-tuple-element.9.refs_1_, bf16[128,128]{1,0:T(8,128)(2,1)S(1)} %collective-permute-done.refs_2_, ...), custom_call_target="tpu_custom_call" | custom-call | tf_op jit(solution)/shard_map/pallas_call | solution.py:111
  14.9 2.4 %all-to-all-start = ((bf16[32,2,72,128]{3,2,1,0:T(8,128)(2,1)}), bf16[32,2,72,128]{3,2,1,0:T(8,128)(2,1)S(1)}, u32[]{:S(2)}, u32[]{:S(2)}) async-start(bf16[32,2,72,128]{3,2,1,0:T(8,128)(2,1)} %shard_map.38), calls=%async_computation | async-start | bytes 2359296 | tf_op jit(solution)/shard_map/all_to_all | solution.py:332
  17.3 26.8 %shard_map.37.t_hbm = bf16[16,9216,128]{2,1,0:T(8,128)(2,1)} custom-call(s32[1]{0:T(128)} %bitcast.1.start_ref, bf16[128,128,512]{2,1,0:T(8,128)(2,1)} %l_hbm.3), custom_call_target="tpu_custom_call" | custom-call | flops 19327352832 | bytes 54525952 | tf_op jit(solution)/shard_map/pallas_call | solution.py:199
  44.1 2.0 %all-to-all-done = bf16[32,2,72,128]{3,2,1,0:T(8,128)(2,1)S(1)} async-done(((bf16[32,2,72,128]{3,2,1,0:T(8,128)(2,1)}), bf16[32,2,72,128]{3,2,1,0:T(8,128)(2,1)S(1)}, u32[]{:S(2)}, u32[]{:S(2)}) %all-to-all-start) | async-done | bytes 1179680 | tf_op jit(solution)/shard_map/all_to_all | solution.py:332
  46.1 1.2 %copy.14 = bf16[8,8,72,128]{3,1,2,0:T(8,128)(2,1)} copy(bf16[8,8,72,128]{3,2,1,0:T(8,128)(2,1)S(1)} %bitcast.39) | data formatting | bytes 2359296
  47.3 39.3 %shard_map.39 = bf16[64,32,128]{2,1,0:T(8,128)(2,1)} custom-call(s32[1]{0:T(128)} %bitcast.1.start_ref, bf16[128,128,512]{2,1,0:T(8,128)(2,1)} %l_hbm.3, bf16[16,9216,128]{2,1,0:T(8,128)(2,1)} %shard_map.37.t_hbm, bf16[64,9216]{1,0:T(8,128)(2,1)} %bitcast.41), custom_call_target="tpu_custom_call" | custom-call | flops 24159191040 | bytes 54525952 | tf_op jit(solution)/shard_map/pallas_call | solution.py:288
  86.7 0.0 copy-start
  86.7 19.0 %all_to_all.10 = bf16[64,32,128]{2,1,0:T(8,128)(2,1)S(1)} all-to-all(bf16[64,32,128]{2,1,0:T(8,128)(2,1)} %shard_map.39), channel_id=1, replica_groups=mesh['pi'=4,'pj'=8] {'pi','pj'}, dimensions={0} | all-to-all | bytes 1048576 | tf_op jit(solution)/shard_map/all_to_all | solution.py:317
  105.7 0.1 convert_reduce_fusion
  105.8 0.0 copy-done
  105.9 0.1 copy.10
  106.0 0.1 copy.9
  106.1 3.5 %collective-permute-start.2 = (bf16[128,128]{0,1:T(8,128)(2,1)S(1)}, bf16[128,128]{0,1:T(8,128)(2,1)S(1)}, u32[]{:S(2)}, u32[]{:S(2)}) collective-permute-start(bf16[128,128]{0,1:T(8,128)(2,1)S(1)} %bitcast.43), channel_id=1, source_target_pairs={{0,0},{1,1},{2,8},{3,9},{4,16},{5,17},{6,24},{7,25},{8,2},{9,3},{1... | collective-permute-start | bytes 98312 | tf_op jit(solution)/shard_map/ppermute | solution.py:32
  109.6 3.0 %collective-permute-start.3 = (bf16[128,128]{0,1:T(8,128)(2,1)S(1)}, bf16[128,128]{0,1:T(8,128)(2,1)S(1)}, u32[]{:S(2)}, u32[]{:S(2)}) collective-permute-start(bf16[128,128]{0,1:T(8,128)(2,1)S(1)} %bitcast.42), channel_id=1, source_target_pairs={{0,1},{1,0},{2,9},{3,8},{4,17},{5,16},{6,25},{7,24},{8,3},{9,2},{1... | collective-permute-start | bytes 98312 | tf_op jit(solution)/shard_map/ppermute | solution.py:32
  112.6 2.0 %collective-permute-done.2 = bf16[128,128]{0,1:T(8,128)(2,1)S(1)} collective-permute-done((bf16[128,128]{0,1:T(8,128)(2,1)S(1)}, bf16[128,128]{0,1:T(8,128)(2,1)S(1)}, u32[]{:S(2)}, u32[]{:S(2)}) %collective-permute-start.2) | collective-permute-done | bytes 32800 | tf_op jit(solution)/shard_map/ppermute | solution.py:32
  114.6 2.0 %collective-permute-done.3 = bf16[128,128]{0,1:T(8,128)(2,1)S(1)} collective-permute-done((bf16[128,128]{0,1:T(8,128)(2,1)S(1)}, bf16[128,128]{0,1:T(8,128)(2,1)S(1)}, u32[]{:S(2)}, u32[]{:S(2)}) %collective-permute-start.3) | collective-permute-done | bytes 32800 | tf_op jit(solution)/shard_map/ppermute | solution.py:32
  116.7 0.7 fusion
  (5 shorter events, 0.1 us)
Async XLA Ops:
  0.8 7.3 %collective-permute-start.1 = (bf16[128,128]{1,0:T(8,128)(2,1)S(1)}, bf16[128,128]{1,0:T(8,128)(2,1)S(1)}, u32[]{:S(2)}, u32[]{:S(2)}) collective-permute-start(bf16[128,128]{1,0:T(8,128)(2,1)S(1)} %get-tuple-element.9.refs_1_), channel_id=1, source_target_pairs={{0,1},{1,0},{2,9},{3,8},{4,17},{5,16},{6,25},{7,24},{8,3},{9,2},{1... | collective-permute-start | bytes 98312 | tf_op jit(solution)/shard_map/ppermute | solution.py:32
  5.6 7.9 %collective-permute-start = (bf16[128,128]{1,0:T(8,128)(2,1)S(1)}, bf16[128,128]{1,0:T(8,128)(2,1)S(1)}, u32[]{:S(2)}, u32[]{:S(2)}) collective-permute-start(bf16[128,128]{1,0:T(8,128)(2,1)S(1)} %get-tuple-element.10.refs_0_), channel_id=1, source_target_pairs={{0,0},{1,1},{2,8},{3,9},{4,16},{5,17},{6,24},{7,25},{8,2},{9,3},{1... | collective-permute-start | bytes 98312 | tf_op jit(solution)/shard_map/ppermute | solution.py:32
  14.9 31.2 %all-to-all-start = ((bf16[32,2,72,128]{3,2,1,0:T(8,128)(2,1)}), bf16[32,2,72,128]{3,2,1,0:T(8,128)(2,1)S(1)}, u32[]{:S(2)}, u32[]{:S(2)}) async-start(bf16[32,2,72,128]{3,2,1,0:T(8,128)(2,1)} %shard_map.38), calls=%async_computation | async-start | bytes 2359296 | tf_op jit(solution)/shard_map/all_to_all | solution.py:332
  86.7 19.1 %copy-start = (f32[2,1,128,128]{3,2,1,0:T(8,128)S(1)}, f32[2,1,128,128]{3,2,1,0:T(8,128)}, u32[]{:S(2)}) copy-start(f32[2,1,128,128]{3,2,1,0:T(8,128)} %param.5) | copy-start | bytes 393220
  106.1 8.5 %collective-permute-start.2 = (bf16[128,128]{0,1:T(8,128)(2,1)S(1)}, bf16[128,128]{0,1:T(8,128)(2,1)S(1)}, u32[]{:S(2)}, u32[]{:S(2)}) collective-permute-start(bf16[128,128]{0,1:T(8,128)(2,1)S(1)} %bitcast.43), channel_id=1, source_target_pairs={{0,0},{1,1},{2,8},{3,9},{4,16},{5,17},{6,24},{7,25},{8,2},{9,3},{1... | collective-permute-start | bytes 98312 | tf_op jit(solution)/shard_map/ppermute | solution.py:32
  109.6 7.0 %collective-permute-start.3 = (bf16[128,128]{0,1:T(8,128)(2,1)S(1)}, bf16[128,128]{0,1:T(8,128)(2,1)S(1)}, u32[]{:S(2)}, u32[]{:S(2)}) collective-permute-start(bf16[128,128]{0,1:T(8,128)(2,1)S(1)} %bitcast.42), channel_id=1, source_target_pairs={{0,1},{1,0},{2,9},{3,8},{4,17},{5,16},{6,25},{7,24},{8,3},{9,2},{1... | collective-permute-start | bytes 98312 | tf_op jit(solution)/shard_map/ppermute | solution.py:32

commit v7 on v6

--- a/solution.py
+++ b/solution.py
@@ -287,7 +287,7 @@
     slots = min(early, 8)
     return pl.pallas_call(
         functools.partial(ladder_kernel, early),
-        out_shape=jax.ShapeDtypeStruct((pairs, rows, width), jnp.bfloat16),
+        out_shape=pltpu.VMEM((pairs, rows, width), jnp.bfloat16),
         grid_spec=pltpu.PrefetchScalarGridSpec(
             num_scalar_prefetch=1,
             grid=(),
@@ -303,7 +303,7 @@
                 pltpu.SemaphoreType.DMA((slots,)),
             ],
         ),
-        compiler_params=pltpu.CompilerParams(vmem_limit_bytes=62 << 20),
+        compiler_params=pltpu.CompilerParams(vmem_limit_bytes=58 << 20),
         cost_estimate=pl.CostEstimate(
             flops=2 * width * size * (late * depth + rows * pairs),
             bytes_accessed=2 * width * width * depth + 2 * early * size * width,
@@ -331,6 +331,8 @@
     copies = packed_copies(amplitudes.reshape(pair_i, width, width), devices)
     weights = lax.all_to_all(copies, BOTH, split_axis=0, concat_axis=0, tiled=True)
     weights = weights.reshape(devices * pair_i, -1)
+    if weights.size <= 1 << 20:
+        weights = pltpu.with_memory_space_constraint(weights, pltpu.VMEM)
     tile = tiles(cholesky, start, early)
     part = collected(ladder(cholesky, tile, weights, start, rows))
     part = jnp.swapaxes(part, 0, 1).reshape(pair_i, width, width)

time: 118 us -> 114 us (0.966)
  Pallas kernels: 67.5 us -> 65.5 us
    pallas_call x1, Pallas kernels: 39.3 us -> 37.3 us  [ladder(): pl.pallas_call(functools.partial(ladder_kernel, early), out_shape=pltpu.V...]
  transfers between devices with their start and end apart: 5 -> 5, of which waited for: 4 -> 4; matrix products, arithmetic and copies ran while one was open for 0% -> 0% of each run, Pallas kernels for 23% -> 24%
where the time goes in v7:
time: 114 us
  Pallas kernels  65.5 us (57%)
  blocking collectives  18.4 us (16%)
  starting transfers between devices  16.2 us (14%)
  waiting for transfers between devices  11.5 us (10%)
  local copies, waits for them, and re-layouts  1.2 us (1%)
    pallas_call x1, Pallas kernels, ladder(): pl.pallas_call(functools.partial(ladder_kernel, early), out_shape=pltpu.V...  37.3 us
    pallas_call x1, Pallas kernels, tiles(): pl.pallas_call(tile_kernel, out_shape=jax.ShapeDtypeStruct((rows, size, w...  26.8 us
    all_to_all x1, blocking collectives, collected(): landed = lax.all_to_all(sums, BOTH, split_axis=0, concat_axis=0, tiled=True)  18.4 us
    ppermute x4, starting transfers between devices, exchanged(): arrived.append(lax.ppermute(sent, BOTH, route))  13.8 us
    ppermute x4, waiting for transfers between devices, exchanged(): arrived.append(lax.ppermute(sent, BOTH, route))  9.54 us
    all_to_all x1, starting transfers between devices, shards(): lax.all_to_all(copies, BOTH, split_axis=0, concat_axis=0, tiled=True)  2.4 us
  transfers between devices with their start and end apart: 5, of which 4 were waited for; matrix products, arithmetic and copies ran while one was open for 0% of the time, Pallas kernels for 24%

profile of v7, /device:TPU:3, one launch (start us, length us, event | category | flops | bytes accessed | tf_op | source)
XLA Modules:
  0.0 113.8 jit_solution(11999508253608950643)
XLA Ops:
  0.0 0.8 dynamic-slice_bitcast_fusion
  0.8 4.8 %collective-permute-start.1 = (bf16[128,128]{1,0:T(8,128)(2,1)S(1)}, bf16[128,128]{1,0:T(8,128)(2,1)S(1)}, u32[]{:S(2)}, u32[]{:S(2)}) collective-permute-start(bf16[128,128]{1,0:T(8,128)(2,1)S(1)} %get-tuple-element.9.refs_1_), channel_id=1, source_target_pairs={{0,1},{1,0},{2,9},{3,8},{4,17},{5,16},{6,25},{7,24},{8,3},{9,2},{1... | collective-permute-start | bytes 98312 | tf_op jit(solution)/shard_map/ppermute | solution.py:32
  5.6 2.5 %collective-permute-start = (bf16[128,128]{1,0:T(8,128)(2,1)S(1)}, bf16[128,128]{1,0:T(8,128)(2,1)S(1)}, u32[]{:S(2)}, u32[]{:S(2)}) collective-permute-start(bf16[128,128]{1,0:T(8,128)(2,1)S(1)} %get-tuple-element.10.refs_0_), channel_id=1, source_target_pairs={{0,0},{1,1},{2,8},{3,9},{4,16},{5,17},{6,24},{7,25},{8,2},{9,3},{1... | collective-permute-start | bytes 98312 | tf_op jit(solution)/shard_map/ppermute | solution.py:32
  8.1 0.0 collective-permute-done.1.refs_3_
  8.1 5.4 %collective-permute-done.refs_2_ = bf16[128,128]{1,0:T(8,128)(2,1)S(1)} collective-permute-done((bf16[128,128]{1,0:T(8,128)(2,1)S(1)}, bf16[128,128]{1,0:T(8,128)(2,1)S(1)}, u32[]{:S(2)}, u32[]{:S(2)}) %collective-permute-start) | collective-permute-done | bytes 32800 | tf_op jit(solution)/shard_map/ppermute | solution.py:32
  13.5 1.4 %shard_map.38 = bf16[32,2,72,128]{3,2,1,0:T(8,128)(2,1)} custom-call(s32[1]{0:T(128)} %bitcast.2.col_ref, bf16[128,128]{1,0:T(8,128)(2,1)S(1)} %get-tuple-element.10.refs_0_, bf16[128,128]{1,0:T(8,128)(2,1)S(1)} %get-tuple-element.9.refs_1_, bf16[128,128]{1,0:T(8,128)(2,1)S(1)} %collective-permute-done.refs_2_, ...), custom_call_target="tpu_custom_call" | custom-call | tf_op jit(solution)/shard_map/pallas_call | solution.py:111
  14.9 2.4 %all-to-all-start = ((bf16[32,2,72,128]{3,2,1,0:T(8,128)(2,1)}), bf16[32,2,72,128]{3,2,1,0:T(8,128)(2,1)S(1)}, u32[]{:S(2)}, u32[]{:S(2)}) async-start(bf16[32,2,72,128]{3,2,1,0:T(8,128)(2,1)} %shard_map.38), calls=%async_computation | async-start | bytes 2359296 | tf_op jit(solution)/shard_map/all_to_all | solution.py:332
  17.3 26.8 %shard_map.37.t_hbm = bf16[16,9216,128]{2,1,0:T(8,128)(2,1)} custom-call(s32[1]{0:T(128)} %bitcast.1.start_ref, bf16[128,128,512]{2,1,0:T(8,128)(2,1)} %l_hbm.3), custom_call_target="tpu_custom_call" | custom-call | flops 19327352832 | bytes 54525952 | tf_op jit(solution)/shard_map/pallas_call | solution.py:199
  44.1 2.0 %all-to-all-done = bf16[32,2,72,128]{3,2,1,0:T(8,128)(2,1)S(1)} async-done(((bf16[32,2,72,128]{3,2,1,0:T(8,128)(2,1)}), bf16[32,2,72,128]{3,2,1,0:T(8,128)(2,1)S(1)}, u32[]{:S(2)}, u32[]{:S(2)}) %all-to-all-start) | async-done | bytes 1179680 | tf_op jit(solution)/shard_map/all_to_all | solution.py:332
  46.1 0.2 copy.14
  46.3 37.3 %shard_map.39 = bf16[64,32,128]{2,1,0:T(8,128)(2,1)S(1)} custom-call(s32[1]{0:T(128)} %bitcast.1.start_ref, bf16[128,128,512]{2,1,0:T(8,128)(2,1)} %l_hbm.3, bf16[16,9216,128]{2,1,0:T(8,128)(2,1)} %shard_map.37.t_hbm, bf16[64,9216]{1,0:T(8,128)(2,1)S(1)} %bitcast.39), custom_call_target="tpu_custom_call" | custom-call | flops 24159191040 | bytes 54525952 | tf_op jit(solution)/shard_map/pallas_call | solution.py:288
  83.6 0.0 copy-start
  83.6 18.4 %all_to_all.10 = bf16[64,32,128]{2,1,0:T(8,128)(2,1)S(1)} all-to-all(bf16[64,32,128]{2,1,0:T(8,128)(2,1)S(1)} %shard_map.39), channel_id=1, replica_groups=mesh['pi'=4,'pj'=8] {'pi','pj'}, dimensions={0} | all-to-all | bytes 1048576 | tf_op jit(solution)/shard_map/all_to_all | solution.py:317
  102.0 0.1 convert_reduce_fusion
  102.1 0.0 copy-done
  102.2 0.1 copy.10
  102.3 0.1 copy.9
  102.4 3.6 %collective-permute-start.2 = (bf16[128,128]{0,1:T(8,128)(2,1)S(1)}, bf16[128,128]{0,1:T(8,128)(2,1)S(1)}, u32[]{:S(2)}, u32[]{:S(2)}) collective-permute-start(bf16[128,128]{0,1:T(8,128)(2,1)S(1)} %bitcast.43), channel_id=1, source_target_pairs={{0,0},{1,1},{2,8},{3,9},{4,16},{5,17},{6,24},{7,25},{8,2},{9,3},{1... | collective-permute-start | bytes 98312 | tf_op jit(solution)/shard_map/ppermute | solution.py:32
  106.1 2.9 %collective-permute-start.3 = (bf16[128,128]{0,1:T(8,128)(2,1)S(1)}, bf16[128,128]{0,1:T(8,128)(2,1)S(1)}, u32[]{:S(2)}, u32[]{:S(2)}) collective-permute-start(bf16[128,128]{0,1:T(8,128)(2,1)S(1)} %bitcast.42), channel_id=1, source_target_pairs={{0,1},{1,0},{2,9},{3,8},{4,17},{5,16},{6,25},{7,24},{8,3},{9,2},{1... | collective-permute-start | bytes 98312 | tf_op jit(solution)/shard_map/ppermute | solution.py:32
  108.9 2.0 %collective-permute-done.2 = bf16[128,128]{0,1:T(8,128)(2,1)S(1)} collective-permute-done((bf16[128,128]{0,1:T(8,128)(2,1)S(1)}, bf16[128,128]{0,1:T(8,128)(2,1)S(1)}, u32[]{:S(2)}, u32[]{:S(2)}) %collective-permute-start.2) | collective-permute-done | bytes 32800 | tf_op jit(solution)/shard_map/ppermute | solution.py:32
  110.9 2.1 %collective-permute-done.3 = bf16[128,128]{0,1:T(8,128)(2,1)S(1)} collective-permute-done((bf16[128,128]{0,1:T(8,128)(2,1)S(1)}, bf16[128,128]{0,1:T(8,128)(2,1)S(1)}, u32[]{:S(2)}, u32[]{:S(2)}) %collective-permute-start.3) | collective-permute-done | bytes 32800 | tf_op jit(solution)/shard_map/ppermute | solution.py:32
  113.1 0.7 fusion
  (5 shorter events, 0.1 us)
Async XLA Ops:
  0.8 7.3 %collective-permute-start.1 = (bf16[128,128]{1,0:T(8,128)(2,1)S(1)}, bf16[128,128]{1,0:T(8,128)(2,1)S(1)}, u32[]{:S(2)}, u32[]{:S(2)}) collective-permute-start(bf16[128,128]{1,0:T(8,128)(2,1)S(1)} %get-tuple-element.9.refs_1_), channel_id=1, source_target_pairs={{0,1},{1,0},{2,9},{3,8},{4,17},{5,16},{6,25},{7,24},{8,3},{9,2},{1... | collective-permute-start | bytes 98312 | tf_op jit(solution)/shard_map/ppermute | solution.py:32
  5.6 7.9 %collective-permute-start = (bf16[128,128]{1,0:T(8,128)(2,1)S(1)}, bf16[128,128]{1,0:T(8,128)(2,1)S(1)}, u32[]{:S(2)}, u32[]{:S(2)}) collective-permute-start(bf16[128,128]{1,0:T(8,128)(2,1)S(1)} %get-tuple-element.10.refs_0_), channel_id=1, source_target_pairs={{0,0},{1,1},{2,8},{3,9},{4,16},{5,17},{6,24},{7,25},{8,2},{9,3},{1... | collective-permute-start | bytes 98312 | tf_op jit(solution)/shard_map/ppermute | solution.py:32
  14.9 31.2 %all-to-all-start = ((bf16[32,2,72,128]{3,2,1,0:T(8,128)(2,1)}), bf16[32,2,72,128]{3,2,1,0:T(8,128)(2,1)S(1)}, u32[]{:S(2)}, u32[]{:S(2)}) async-start(bf16[32,2,72,128]{3,2,1,0:T(8,128)(2,1)} %shard_map.38), calls=%async_computation | async-start | bytes 2359296 | tf_op jit(solution)/shard_map/all_to_all | solution.py:332
  83.6 18.6 %copy-start = (f32[2,1,128,128]{3,2,1,0:T(8,128)S(1)}, f32[2,1,128,128]{3,2,1,0:T(8,128)}, u32[]{:S(2)}) copy-start(f32[2,1,128,128]{3,2,1,0:T(8,128)} %param.5) | copy-start | bytes 393220
  102.4 8.5 %collective-permute-start.2 = (bf16[128,128]{0,1:T(8,128)(2,1)S(1)}, bf16[128,128]{0,1:T(8,128)(2,1)S(1)}, u32[]{:S(2)}, u32[]{:S(2)}) collective-permute-start(bf16[128,128]{0,1:T(8,128)(2,1)S(1)} %bitcast.43), channel_id=1, source_target_pairs={{0,0},{1,1},{2,8},{3,9},{4,16},{5,17},{6,24},{7,25},{8,2},{9,3},{1... | collective-permute-start | bytes 98312 | tf_op jit(solution)/shard_map/ppermute | solution.py:32
  106.1 7.0 %collective-permute-start.3 = (bf16[128,128]{0,1:T(8,128)(2,1)S(1)}, bf16[128,128]{0,1:T(8,128)(2,1)S(1)}, u32[]{:S(2)}, u32[]{:S(2)}) collective-permute-start(bf16[128,128]{0,1:T(8,128)(2,1)S(1)} %bitcast.42), channel_id=1, source_target_pairs={{0,1},{1,0},{2,9},{3,8},{4,17},{5,16},{6,25},{7,24},{8,3},{9,2},{1... | collective-permute-start | bytes 98312 | tf_op jit(solution)/shard_map/ppermute | solution.py:32
